TPU v7x, 512 devices: a whole 4x4x16 slice. The times are simulated.
512 devices in a mesh: ctx: 32 (over z, core), rep: 16 (over y, x).
Axes of the slice: x: 4, y: 4, z: 16, core: 2. Of those that a mesh axis runs over, the one named last changes fastest.
Arguments:
- queries: bfloat16 [512, 8192], P(None, 'ctx'), may hold values from -6 to 6
- keys: bfloat16 [65536, 1024], P(('ctx', 'rep')), may hold values from -6 to 6
- values: bfloat16 [65536, 1024], P(('ctx', 'rep')), may hold values from -6 to 6
- forward_output: bfloat16 [512, 8192], P(None, 'ctx'), may hold values from -6 to 6
- output_gradient: bfloat16 [512, 8192], P(None, 'ctx'), may hold values from -6 to 6
- log_sum_norm: float32 [64, 512], P('ctx'), may hold values from 3 to 5
- block_attend_mask: int32 [64, 4, 512], P('ctx'), may hold values from 0 to 1, as said below
Outputs:
- grad_queries: bfloat16 [512, 8192], P('rep', 'ctx')
- key_gradient: bfloat16 [65536, 1024], P(('ctx', 'rep'))
- value_gradient: bfloat16 [65536, 1024], P(('ctx', 'rep'))
Inputs may be any that keep to these rules, and one draw needn't show every extreme that they name: `block_attend_mask`: 1 where a query block of a query head attends a key block of 128 tokens, else 0; how many key blocks are attended differs from head to head.
All inputs are finite; a program needn't handle non-finite values.
Results may differ from a plain program's by a relative error of at most 0.007.
Values may be sent and summed in bfloat16 or wider, within the bound.
No kernel may reach another device: no remote copies, remote signals or barrier semaphores. Data moves between devices by JAX's collectives and lax.ppermute only.
A program may use at most 64 MiB of HBM per device.

v0:
```python
import jax
import jax.numpy as jnp
from jax import lax
from jax.sharding import PartitionSpec as P

KEY_VALUE_HEADS = 8
HEAD_SIZE = 128
BLK = 128
SLAB_QUERIES = 512


def side_by_side(arrays, axis, split_dim, concat_dim, along):
    ends, at = ([], 0)
    for a in arrays[:-1]:
        at += a.shape[along]
        ends.append(at)
    both = jnp.concatenate(arrays, axis=along)
    return tuple(
        jnp.split(
            lax.all_to_all(both, axis, split_axis=split_dim, concat_axis=concat_dim, tiled=True),
            ends,
            axis=along,
        )
    )


def partner_2(value, axis, apart):
    mask = 2**apart
    pairs = [(source, source ^ mask) for source in range(lax.axis_size(axis))]
    return lax.ppermute(value, axis, pairs)


def split_up(shard, dim, count):
    before, after = (shard.shape[:dim], shard.shape[dim + 1 :])
    return jnp.moveaxis(shard.reshape(*before, count, -1, *after), dim, 0)


def sum_at_owner(shard, axis, dim):
    count = lax.axis_size(axis)
    tiles = lax.all_to_all(split_up(shard, dim, count), axis, 0, 0, tiled=True)
    return jnp.sum(tiles, axis=0)


def on_device(
    queries, keys, values, forward_output, output_gradient, log_sum_norm, block_attend_mask
):
    context_length = lax.axis_size("ctx")
    rep_size = lax.axis_size("rep")
    group_width = context_length // KEY_VALUE_HEADS
    heads_dev = queries.shape[1] // HEAD_SIZE
    keys_local_share = keys.shape[0]
    sub_keys = keys_local_share // group_width
    span_len = context_length * keys_local_share
    block_count = span_len // BLK
    query_block_count = SLAB_QUERIES // BLK
    softmax_scale = HEAD_SIZE ** (-0.5)
    ctx_pos = lax.axis_index("ctx")
    rep_pos = lax.axis_index("rep")
    bit_total = group_width.bit_length() - 1

    def split_shares(number_array):
        shares = number_array.reshape(group_width, sub_keys, KEY_VALUE_HEADS, HEAD_SIZE).transpose(
            1, 2, 0, 3
        )
        return shares.reshape(sub_keys, context_length, HEAD_SIZE)

    arrived_keys, arrived_values = side_by_side(
        (split_shares(keys), split_shares(values)), "ctx", 1, 0, 2
    )
    holding = jnp.stack(
        [
            arrived_keys.reshape(context_length, 1, sub_keys, HEAD_SIZE),
            arrived_values.reshape(context_length, 1, sub_keys, HEAD_SIZE),
        ]
    )
    for bit_number in range(bit_total):
        partner = partner_2(holding, "ctx", bit_number)
        high_bit = ctx_pos // (1 << bit_number) % 2
        holding = jnp.where(
            high_bit == 0,
            jnp.concatenate([holding, partner], axis=2),
            jnp.concatenate([partner, holding], axis=2),
        )
    key_span = holding[0].reshape(span_len, HEAD_SIZE)
    value_span = holding[1].reshape(span_len, HEAD_SIZE)
    query_heads = queries.reshape(SLAB_QUERIES, heads_dev, HEAD_SIZE).transpose(1, 0, 2)
    cotan_heads = output_gradient.reshape(SLAB_QUERIES, heads_dev, HEAD_SIZE).transpose(1, 0, 2)
    row_dots = jnp.sum(
        (output_gradient.astype(jnp.float32) * forward_output.astype(jnp.float32)).reshape(
            SLAB_QUERIES, heads_dev, HEAD_SIZE
        ),
        axis=2,
    ).T
    mask_local = block_attend_mask.reshape(
        heads_dev, query_block_count, context_length, rep_size, keys_local_share // BLK
    )
    mask_span = lax.dynamic_index_in_dim(mask_local, rep_pos, 3, keepdims=False).reshape(
        heads_dev, query_block_count, block_count
    )
    tile_count = 4
    key_blocks = key_span.reshape(block_count, BLK, HEAD_SIZE)
    value_blocks = value_span.reshape(block_count, BLK, HEAD_SIZE)
    start_totals = (
        jnp.zeros((block_count, BLK, HEAD_SIZE), jnp.float32),
        jnp.zeros((block_count, BLK, HEAD_SIZE), jnp.float32),
        jnp.zeros((heads_dev, SLAB_QUERIES, HEAD_SIZE), jnp.float32),
    )
    used_blocks = jnp.max(mask_span, axis=(0, 1))
    block_order = jnp.argsort(1 - used_blocks, stable=True)
    live_count = jnp.sum(used_blocks)
    turn_total = (live_count + tile_count - 1) // tile_count

    def one_turn(turn, carry):
        key_total, value_total, query_total = carry
        picked = lax.dynamic_slice_in_dim(block_order, turn * tile_count, tile_count)
        live_flags = (
            turn * tile_count + jnp.arange(tile_count, dtype=jnp.int32) < live_count
        ).astype(jnp.int32)
        key_tile = jnp.take(key_blocks, picked, axis=0).reshape(tile_count * BLK, HEAD_SIZE)
        value_tile = jnp.take(value_blocks, picked, axis=0).reshape(tile_count * BLK, HEAD_SIZE)
        mask_tile = jnp.take(mask_span, picked, axis=2) * live_flags[None, None, :]
        mask_full = jnp.broadcast_to(
            mask_tile[:, :, None, :, None].astype(jnp.float32),
            (heads_dev, query_block_count, BLK, tile_count, BLK),
        ).reshape(heads_dev, SLAB_QUERIES, tile_count * BLK)
        scores = (
            jnp.einsum("hqd,kd->hqk", query_heads, key_tile, preferred_element_type=jnp.float32)
            * softmax_scale
        )
        weights_f = jnp.exp(scores - log_sum_norm[:, :, None]) * mask_full
        weights_b = weights_f.astype(jnp.bfloat16)
        grad_weights = jnp.einsum(
            "hqd,kd->hqk", cotan_heads, value_tile, preferred_element_type=jnp.float32
        )
        grad_scores = (weights_f * (grad_weights - row_dots[:, :, None])).astype(jnp.bfloat16)
        value_part = jnp.einsum(
            "hqk,hqd->kd", weights_b, cotan_heads, preferred_element_type=jnp.float32
        ).reshape(tile_count, BLK, HEAD_SIZE)
        key_part = jnp.einsum(
            "hqk,hqd->kd", grad_scores, query_heads, preferred_element_type=jnp.float32
        ).reshape(tile_count, BLK, HEAD_SIZE)
        query_total = query_total + jnp.einsum(
            "hqk,kd->hqd", grad_scores, key_tile, preferred_element_type=jnp.float32
        )
        key_total = key_total.at[picked].add(key_part)
        value_total = value_total.at[picked].add(value_part)
        return (key_total, value_total, query_total)

    key_total, value_total, query_total = lax.fori_loop(0, turn_total, one_turn, start_totals)
    key_scaled = key_total * softmax_scale
    query_terms = (
        (query_total * softmax_scale)
        .transpose(1, 0, 2)
        .reshape(SLAB_QUERIES, heads_dev * HEAD_SIZE)
    )
    grad_queries = sum_at_owner(query_terms, "rep", 0).astype(jnp.bfloat16)
    grad_parts = jnp.stack([key_scaled, value_total]).astype(jnp.bfloat16)
    holding = grad_parts.reshape(2, context_length, group_width, sub_keys, HEAD_SIZE)
    dest_count = group_width
    for bit_number in range(bit_total):
        dest_count = dest_count // 2
        halves = holding.reshape(2, context_length, dest_count, 2, sub_keys, HEAD_SIZE)
        own_bit = ctx_pos // (1 << bit_number) % 2
        kept_half = lax.dynamic_index_in_dim(halves, own_bit, 3, keepdims=False)
        sent_half = lax.dynamic_index_in_dim(halves, 1 - own_bit, 3, keepdims=False)
        partner_half = partner_2(sent_half, "ctx", bit_number)
        holding = (kept_half.astype(jnp.float32) + partner_half.astype(jnp.float32)).astype(
            jnp.bfloat16
        )
    own_sum = holding.reshape(2, context_length, sub_keys, HEAD_SIZE)
    returned_value = lax.all_to_all(own_sum, "ctx", split_axis=1, concat_axis=1, tiled=True)
    joined_result = returned_value.reshape(2, KEY_VALUE_HEADS, keys_local_share, HEAD_SIZE)
    closing_gradients = jnp.transpose(joined_result, (0, 2, 1, 3)).reshape(
        2, keys_local_share, KEY_VALUE_HEADS * HEAD_SIZE
    )
    return (grad_queries, closing_gradients[0], closing_gradients[1])


def solution(mesh):
    in_specs = (
        P(None, "ctx"),
        P(("ctx", "rep"), None),
        P(("ctx", "rep"), None),
        P(None, "ctx"),
        P(None, "ctx"),
        P("ctx", None),
        P("ctx", None, None),
    )
    out_specs = (P("rep", "ctx"), P(("ctx", "rep"), None), P(("ctx", "rep"), None))
    return jax.shard_map(
        on_device, mesh=mesh, in_specs=in_specs, out_specs=out_specs, check_vma=False
    )
```

profile of v0, /device:TPU:1, one launch (start us, length us, event | category | flops | bytes accessed | tf_op | source)
XLA Modules:
  0.0 270.7 jit_solution(9343792079820551747)
XLA Ops:
  0.6 1.0 copy.59
  1.7 1.0 copy.60
  2.9 50.1 %all_to_all.28 = bf16[32,32,256]{2,0,1:T(8,128)(2,1)S(1)} all-to-all(bf16[32,32,256]{2,0,1:T(8,128)(2,1)S(1)} %pad_maximum_fusion), channel_id=1, replica_groups=mesh['ctx'=32,'rep'=16] {'ctx'}, dimensions={1} | all-to-all | bytes 1048576 | tf_op jit(solution)/shard_map/all_to_all | solution.py:20
  53.0 2.5 collective-permute-start
  55.6 1.5 collective-permute-done
  57.2 1.9 collective-permute-start.1
  63.1 1.7 sort.17
  64.8 18.8 %collective-permute-done.1 = bf16[2,32,2,32,128]{4,3,2,1,0:T(8,128)(2,1)} collective-permute-done((bf16[2,32,2,32,128]{4,3,2,1,0:T(8,128)(2,1)S(1)}, bf16[2,32,2,32,128]{4,3,2,1,0:T(8,128)(2,1)}, u32[]{:S(2)}, u32[]{:S(2)}) %collective-permute-start.1) | collective-permute-done | bytes 1048608 | tf_op jit(solution)/shard_map/ppermute | solution.py:30
  83.5 1.8 maximum_select_fusion
  85.4 1.7 fusion.10
  87.1 1.5 broadcast.67.clone
  88.7 1.6 broadcast.67
  90.3 47.8 %while.14 = (s32[]{:T(128)}, f32[32,128,128]{2,1,0:T(8,128)}, f32[32,128,128]{2,1,0:T(8,128)}, f32[2,512,128]{2,1,0:T(8,128)S(1)}, s32[]{:T(128)}, /*index=5*/s3...) while((s32[]{:T(128)}, f32[32,128,128]{2,1,0:T(8,128)}, ...), condition=%wide.region_7.9_spmd, body=%wide.region_4.8_spmd.sunk | while | flops 675153024 | bytes 23475468 | solution.py:149
  90.3 0.7 compare_and_fusion.2
  91.7 1.8 gather_fusion.2
  93.5 1.8 gather_fusion.1
  95.7 1.9 reshape.185
  97.6 2.1 bitcast_multiply_fusion.3
  101.6 2.3 scatter_fusion
  103.9 2.3 scatter_fusion.1
  106.2 0.7 compare_and_fusion.2
  107.6 1.8 gather_fusion.2
  109.4 1.8 gather_fusion.1
  111.6 1.9 reshape.185
  113.5 2.1 bitcast_multiply_fusion.3
  117.5 2.3 scatter_fusion
  119.8 2.3 scatter_fusion.1
  122.1 0.7 compare_and_fusion.2
  123.5 1.8 gather_fusion.2
  125.3 1.8 gather_fusion.1
  127.6 1.9 reshape.185
  129.5 2.1 bitcast_multiply_fusion.3
  133.4 2.3 scatter_fusion
  135.8 2.3 scatter_fusion.1
  138.1 2.0 multiply_convert_fusion
  140.5 1.1 fusion.5
  141.6 19.1 %collective-permute-start.2 = (bf16[2,32,2,32,128]{4,3,2,1,0:T(8,128)(2,1)}, bf16[2,32,2,32,128]{4,3,2,1,0:T(8,128)(2,1)}, u32[]{:S(2)}, u32[]{:S(2)}) collective-permute-start(bf16[2,32,2,32,128]{4,3,2,1,0:T(8,128)(2,1)} %fusion.5), channel_id=1, source_target_pairs={{0,16},{16,0},{32,48},{48,32},{64,80},{80,64},{96,112},{112,96},{1... | collective-permute-start | bytes 3145736 | tf_op jit(solution)/shard_map/ppermute | solution.py:30
  160.7 2.6 collective-permute-done.2
  163.3 1.6 fusion.3
  165.0 17.0 %collective-permute-start.3 = (bf16[2,32,1,32,128]{4,3,2,1,0:T(8,128)(2,1)S(1)}, bf16[2,32,1,32,128]{4,3,2,1,0:T(8,128)(2,1)S(1)}, u32[]{:S(2)}, u32[]{:S(2)}) collective-permute-start(bf16[2,32,1,32,128]{4,3,2,1,0:T(8,128)(2,1)S(1)} %constant_dynamic-slice_fusion), channel_id=1, source_target_pairs={{0,32},{16,48},{32,0},{48,16},{64,96},{80,112},{96,64},{112,80},{1... | collective-permute-start | bytes 1572872 | tf_op jit(solution)/shard_map/ppermute | solution.py:30
  182.5 1.2 reshape_reshape.4
  183.8 22.6 %all-to-all-start.1 = ((f32[16,32,256]{2,1,0:T(8,128)}), f32[16,32,256]{2,1,0:T(8,128)S(1)}, u32[]{:S(2)}, u32[]{:S(2)}) async-start(f32[16,32,256]{2,1,0:T(8,128)} %reshape_reshape.4), calls=%async_computation.1 | async-start | bytes 1048576 | tf_op jit(solution)/shard_map/all_to_all | solution.py:40
  206.5 0.9 copy.51
  207.4 9.7 %all-to-all-done.1 = f32[16,32,256]{2,1,0:T(8,128)S(1)} async-done(((f32[16,32,256]{2,1,0:T(8,128)}), f32[16,32,256]{2,1,0:T(8,128)S(1)}, u32[]{:S(2)}, u32[]{:S(2)}) %all-to-all-start.1) | async-done | bytes 524320 | tf_op jit(solution)/shard_map/all_to_all | solution.py:40
  217.0 18.0 %all-to-all-start.2 = ((bf16[2,32,32,128]{3,2,0,1:T(8,128)(2,1)}), bf16[2,32,32,128]{3,2,0,1:T(8,128)(2,1)S(1)}, u32[]{:S(2)}, u32[]{:S(2)}) async-start(bf16[2,32,32,128]{3,2,0,1:T(8,128)(2,1)} %copy.51), calls=%async_computation.2 | async-start | bytes 1048576 | tf_op jit(solution)/shard_map/all_to_all | solution.py:171
  235.7 32.9 %all-to-all-done.2 = bf16[2,32,32,128]{3,2,0,1:T(8,128)(2,1)S(1)} async-done(((bf16[2,32,32,128]{3,2,0,1:T(8,128)(2,1)}), bf16[2,32,32,128]{3,2,0,1:T(8,128)(2,1)S(1)}, u32[]{:S(2)}, u32[]{:S(2)}) %all-to-all-start.2) | async-done | bytes 524320 | tf_op jit(solution)/shard_map/all_to_all | solution.py:171
  268.9 0.9 copy.56
  269.9 0.9 copy.55
  (79 shorter events, 14.4 us)
Async XLA Ops:
  52.9 6.3 %copy-start.7 = (s32[2,4,512]{2,1,0:T(4,128)S(1)}, s32[2,4,512]{2,1,0:T(4,128)}, u32[]{:S(2)}) copy-start(s32[2,4,512]{2,1,0:T(4,128)} %param.17) | copy-start | bytes 49156
  53.0 8.4 %copy-start.4 = (bf16[512,256]{1,0:T(8,128)(2,1)S(1)}, bf16[512,256]{1,0:T(8,128)(2,1)}, u32[]{:S(2)}) copy-start(bf16[512,256]{1,0:T(8,128)(2,1)} %param.11) | copy-start | bytes 786436
  53.0 8.6 %copy-start.3 = (bf16[512,256]{1,0:T(8,128)(2,1)S(1)}, bf16[512,256]{1,0:T(8,128)(2,1)}, u32[]{:S(2)}) copy-start(bf16[512,256]{1,0:T(8,128)(2,1)} %param.15) | copy-start | bytes 786436
  53.0 4.1 %collective-permute-start = (bf16[2,32,1,32,128]{4,3,2,1,0:T(8,128)(2,1)S(1)}, bf16[2,32,1,32,128]{4,3,2,1,0:T(8,128)(2,1)S(1)}, u32[]{:S(2)}, u32[]{:S(2)}) collective-permute-start(bf16[2,32,1,32,128]{4,3,2,1,0:T(8,128)(2,1)S(1)} %pad_maximum_fusion.1), channel_id=1, source_target_pairs={{0,16},{16,0},{32,48},{48,32},{64,80},{80,64},{96,112},{112,96},{1... | collective-permute-start | bytes 1572872 | tf_op jit(solution)/shard_map/ppermute | solution.py:30
  55.6 6.4 %copy-start.5 = (bf16[512,256]{1,0:T(8,128)(2,1)S(1)}, bf16[512,256]{1,0:T(8,128)(2,1)}, u32[]{:S(2)}) copy-start(bf16[512,256]{1,0:T(8,128)(2,1)} %param.14) | copy-start | bytes 786436
  57.2 26.3 %collective-permute-start.1 = (bf16[2,32,2,32,128]{4,3,2,1,0:T(8,128)(2,1)S(1)}, bf16[2,32,2,32,128]{4,3,2,1,0:T(8,128)(2,1)}, u32[]{:S(2)}, u32[]{:S(2)}) collective-permute-start(bf16[2,32,2,32,128]{4,3,2,1,0:T(8,128)(2,1)S(1)} %maximum_select_fusion.1), channel_id=1, source_target_pairs={{0,32},{16,48},{32,0},{48,16},{64,96},{80,112},{96,64},{112,80},{1... | collective-permute-start | bytes 3145736 | tf_op jit(solution)/shard_map/ppermute | solution.py:30
  87.1 3.2 %copy-start.6 = (f32[2,512]{1,0:T(2,128)S(1)}, f32[2,512]{1,0:T(2,128)}, u32[]{:S(2)}) copy-start(f32[2,512]{1,0:T(2,128)} %param.16) | copy-start | bytes 12292
  138.1 2.2 copy-start
  141.6 21.7 %collective-permute-start.2 = (bf16[2,32,2,32,128]{4,3,2,1,0:T(8,128)(2,1)}, bf16[2,32,2,32,128]{4,3,2,1,0:T(8,128)(2,1)}, u32[]{:S(2)}, u32[]{:S(2)}) collective-permute-start(bf16[2,32,2,32,128]{4,3,2,1,0:T(8,128)(2,1)} %fusion.5), channel_id=1, source_target_pairs={{0,16},{16,0},{32,48},{48,32},{64,80},{80,64},{96,112},{112,96},{1... | collective-permute-start | bytes 3145736 | tf_op jit(solution)/shard_map/ppermute | solution.py:30
  164.9 17.2 %copy-start.1 = (bf16[2,32,2,32,128]{4,3,2,1,0:T(8,128)(2,1)}, bf16[2,32,2,32,128]{4,3,2,1,0:T(8,128)(2,1)S(1)}, u32[]{:S(2)}) copy-start(bf16[2,32,2,32,128]{4,3,2,1,0:T(8,128)(2,1)S(1)} %fusion.3) | copy-start | bytes 3145732
  165.0 41.4 %collective-permute-start.3 = (bf16[2,32,1,32,128]{4,3,2,1,0:T(8,128)(2,1)S(1)}, bf16[2,32,1,32,128]{4,3,2,1,0:T(8,128)(2,1)S(1)}, u32[]{:S(2)}, u32[]{:S(2)}) collective-permute-start(bf16[2,32,1,32,128]{4,3,2,1,0:T(8,128)(2,1)S(1)} %constant_dynamic-slice_fusion), channel_id=1, source_target_pairs={{0,32},{16,48},{32,0},{48,16},{64,96},{80,112},{96,64},{112,80},{1... | collective-permute-start | bytes 1572872 | tf_op jit(solution)/shard_map/ppermute | solution.py:30
  182.5 23.8 %copy-start.2 = (bf16[2,32,2,32,128]{4,3,2,1,0:T(8,128)(2,1)S(1)}, bf16[2,32,2,32,128]{4,3,2,1,0:T(8,128)(2,1)}, u32[]{:S(2)}) copy-start(bf16[2,32,2,32,128]{4,3,2,1,0:T(8,128)(2,1)} %copy-done.1) | copy-start | bytes 3145732
  183.8 33.3 %all-to-all-start.1 = ((f32[16,32,256]{2,1,0:T(8,128)}), f32[16,32,256]{2,1,0:T(8,128)S(1)}, u32[]{:S(2)}, u32[]{:S(2)}) async-start(f32[16,32,256]{2,1,0:T(8,128)} %reshape_reshape.4), calls=%async_computation.1 | async-start | bytes 1048576 | tf_op jit(solution)/shard_map/all_to_all | solution.py:40
  217.0 51.6 %all-to-all-start.2 = ((bf16[2,32,32,128]{3,2,0,1:T(8,128)(2,1)}), bf16[2,32,32,128]{3,2,0,1:T(8,128)(2,1)S(1)}, u32[]{:S(2)}, u32[]{:S(2)}) async-start(bf16[2,32,32,128]{3,2,0,1:T(8,128)(2,1)} %copy.51), calls=%async_computation.2 | async-start | bytes 1048576 | tf_op jit(solution)/shard_map/all_to_all | solution.py:171
where the time goes:
time: 273 us; the launch traced here: 271 us
  starting transfers between devices  81.2 us (30%)
  waiting for transfers between devices  65.4 us (24%)
  blocking collectives  50.1 us (18%)
  local copies, waits for them, and re-layouts  32.7 us (12%)
  other arithmetic  27.5 us (10%)
  matrix products  11.9 us (4%)
    all_to_all x1, blocking collectives, side_by_side(): lax.all_to_all(both, axis, split_axis=split_dim, concat_axis=concat_dim,...  50.1 us
    ppermute x4, starting transfers between devices, partner_2(): return lax.ppermute(value, axis, pairs)  40.6 us
    all_to_all x1, waiting for transfers between devices, on_device(): lax.all_to_all(own_sum, 'ctx', split_axis=1, concat_axis=1, tiled=True)  32.9 us
    ppermute x4, waiting for transfers between devices, partner_2(): return lax.ppermute(value, axis, pairs)  22.9 us
    all_to_all x1, starting transfers between devices, sum_at_owner(): tiles = lax.all_to_all(split_up(shard, dim, count), axis, 0, 0, tiled=True)  22.6 us
    all_to_all x1, starting transfers between devices, on_device(): lax.all_to_all(own_sum, 'ctx', split_axis=1, concat_axis=1, tiled=True)  18 us
    all_to_all x1, waiting for transfers between devices, sum_at_owner(): tiles = lax.all_to_all(split_up(shard, dim, count), axis, 0, 0, tiled=True)  9.65 us
    scatter-add x3, other arithmetic, one_turn(): value_total = value_total.at[picked].add(value_part)  6.91 us
  transfers between devices with their start and end apart: 6, of which 5 were waited for; matrix products, arithmetic and copies ran while one was open for 3% of the time, Pallas kernels for 0%

commit v1 on v0

v1 whole, which is shorter than its diff:
```python
import math

import jax
import jax.numpy as jnp
from jax import lax
from jax.experimental import pallas as pl
from jax.experimental.pallas import tpu as pltpu
from jax.sharding import Mesh, PartitionSpec as P


KEY_VALUE_HEADS = 8
HEAD_SIZE = 128
BLK = 128
SLAB_QUERIES = 512
Z, CORES, Y, X = 16, 2, 4, 4
SLOTS = 4
HALF = BLK // 2
TILE = SLAB_QUERIES // (Y * X)
PACKED = 2 * SLAB_QUERIES + 32
PICK = 4
LOG2E = math.log2(math.e)
NEVER = -1e30
f32, bf16 = jnp.float32, jnp.bfloat16


def dot(a, b, dims):
    return lax.dot_general(a, b, (dims, ((), ())), preferred_element_type=f32)


def prepare_kernel(rep, queries, keys, values, output, cotangent, norm, mask, kv, packed):
    for g in range(KEY_VALUE_HEADS):
        lanes = slice(g * HEAD_SIZE, (g + 1) * HEAD_SIZE)
        for half in range(2):
            rows = slice(half * HALF, (half + 1) * HALF)
            kv[2 * g + half, 0] = keys[rows, lanes]
            kv[2 * g + half, 1] = values[rows, lanes]
    packed[:SLAB_QUERIES] = queries[...]
    packed[SLAB_QUERIES:2 * SLAB_QUERIES] = cotangent[...]
    rows = []
    for l in range(2):
        lanes = slice(l * HEAD_SIZE, (l + 1) * HEAD_SIZE)
        product = cotangent[:, lanes].astype(f32) * output[:, lanes].astype(f32)
        rows.append(jnp.sum(product.T, axis=0, keepdims=True))
    rows += [norm[l:l + 1] * (-LOG2E) for l in range(2)]
    wide = 2 * HEAD_SIZE
    exact = jnp.concatenate([r[:, i * wide:(i + 1) * wide] for r in rows for i in range(2)], axis=0)
    high = exact.astype(bf16).astype(f32)
    block = lax.broadcasted_iota(jnp.int32, (CORES * Z * Y * X, HEAD_SIZE), 0)
    lane = lax.broadcasted_iota(jnp.int32, (CORES * Z * Y * X, HEAD_SIZE), 1)
    wanted = ((lane % Z) * CORES + lane // Z) * (Y * X) + rep[0]
    pick = jnp.where((block == wanted) & (lane < CORES * Z), 1.0, 0.0).astype(bf16)
    attend = jnp.concatenate([mask[0], mask[1]], axis=0).astype(f32).astype(bf16)
    picked = dot(attend, pick, ((1,), (0,)))
    zeros = jnp.zeros((8, HEAD_SIZE), f32)
    picked = jnp.concatenate([picked, zeros], axis=1)
    aux = jnp.concatenate([high, exact - high, picked, jnp.zeros((8, wide), f32)], axis=0)
    packed[2 * SLAB_QUERIES:] = aux.astype(bf16)


def prepare(rep, *arrays):
    vmem = pl.BlockSpec(memory_space=pltpu.VMEM)
    return pl.pallas_call(
        prepare_kernel,
        out_shape=(
            jax.ShapeDtypeStruct((Z, 2, HALF, HEAD_SIZE), bf16),
            jax.ShapeDtypeStruct((PACKED, 2 * HEAD_SIZE), bf16),
        ),
        in_specs=[pl.BlockSpec(memory_space=pltpu.SMEM)] + [vmem] * 7,
        out_specs=(vmem, vmem),
        compiler_params=pltpu.CompilerParams(vmem_limit_bytes=12 * 2**20),
        name="prepare",
    )(rep, *arrays)


def to_row_kernel(place, keep, got, own, *sent):
    for d, out in enumerate((own, *sent)):
        for y in range(Y):
            at = pl.multiple_of((y * X + lax.rem(place[0] + d, X)) * TILE, TILE)
            for s in range(2):
                total = keep[s, pl.ds(at, TILE), :] + got[s, pl.ds(at, TILE), :].astype(f32)
                out[s, y] = total.astype(out.dtype)


def to_tile_kernel(place, keep, got1, got2, got3, own, *sent):
    for d, out in enumerate((own, *sent)):
        at = lax.rem(place[0] + d, Y)
        for s in range(2):
            total = keep[s, at]
            for got in (got1, got2, got3):
                total = total + got[s, at].astype(f32)
            out[s] = total.astype(out.dtype)


def reduce_step(kernel, place, shape, *arrays):
    vmem = pl.BlockSpec(memory_space=pltpu.VMEM)
    return pl.pallas_call(
        kernel,
        out_shape=(jax.ShapeDtypeStruct(shape, f32),) + (jax.ShapeDtypeStruct(shape, bf16),) * 3,
        in_specs=[pl.BlockSpec(memory_space=pltpu.SMEM)] + [vmem] * len(arrays),
        out_specs=(vmem,) * 4,
        compiler_params=pltpu.CompilerParams(vmem_limit_bytes=8 * 2**20),
    )(place, *arrays)


def around(value, axis, distance):
    return lax.ppermute(value, axis, [(i, (i + distance) % 4) for i in range(4)])


def attention_kernel(mask, kv, x0, x1, x2, x3, dkv, keep, send,
                     order, qs, gs, norm, dots, kbuf, vbuf, dk, dv, dq):
    scale = HEAD_SIZE ** -0.5
    for s, x in enumerate((x0, x1, x2, x3)):
        aux = x[2 * SLAB_QUERIES:].astype(f32)
        aux = aux[:8] + aux[8:16]
        for l in range(2):
            lanes = slice(l * HEAD_SIZE, (l + 1) * HEAD_SIZE)
            qs[2 * s + l] = x[:SLAB_QUERIES, lanes]
            gs[2 * s + l] = x[SLAB_QUERIES:2 * SLAB_QUERIES, lanes]
            dots[2 * s + l] = jnp.concatenate([aux[2 * l:2 * l + 1], aux[2 * l + 1:2 * l + 2]], axis=1)
            norm[2 * s + l] = jnp.concatenate([aux[2 * l + 4:2 * l + 5], aux[2 * l + 5:2 * l + 6]], axis=1)
    dk[...] = jnp.zeros_like(dk)
    dv[...] = jnp.zeros_like(dv)
    dq[...] = jnp.zeros_like(dq)

    def head(h, _):
        live = []
        for b in range(Z):
            any_of = mask[h * 4, b]
            for qb in range(1, 4):
                any_of = any_of | mask[h * 4 + qb, b]
            live.append(jnp.minimum(any_of, 1))
        n = jnp.int32(0)
        for b in range(Z):
            order[n] = b
            n = n + live[b]
        total = n
        for b in range(Z):
            order[n] = b
            n = n + (1 - live[b])

        def turn(t, _):
            picked = [order[t * PICK + j] for j in range(PICK)]
            rows = []
            for j, i in enumerate(picked):
                kbuf[pl.ds(j * HALF, HALF), :] = kv[i, 0]
                vbuf[pl.ds(j * HALF, HALF), :] = kv[i, 1]
                row = jnp.concatenate(
                    [
                        jnp.where(mask[h * 4 + qb, i] > 0, norm[h, :, pl.ds(qb * BLK, BLK)], NEVER)
                        for qb in range(4)
                    ],
                    axis=1,
                )
                rows.append(jnp.broadcast_to(row, (HALF, SLAB_QUERIES)))
            bias = jnp.concatenate(rows, axis=0)
            q, g = qs[h], gs[h]
            scores = dot(kbuf[...], q, ((1,), (1,)))
            w = jnp.exp2(scores * (scale * LOG2E) + bias)
            gw = dot(vbuf[...], g, ((1,), (1,)))
            ds = (w * (gw - dots[h])).astype(bf16)
            dv_part = dot(w.astype(bf16), g, ((1,), (0,)))
            dk_part = dot(ds, q, ((1,), (0,)))
            for j, i in enumerate(picked):
                dv[i] += dv_part[j * HALF:(j + 1) * HALF]
                dk[i] += dk_part[j * HALF:(j + 1) * HALF]
            dq[h] += dot(kbuf[...], ds, ((0,), (0,)))
            return 0

        lax.fori_loop(0, (total + PICK - 1) // PICK, turn, 0)
        return 0

    lax.fori_loop(0, 2 * SLOTS, head, 0)
    dkv[:, 0] = (dk[...] * scale).astype(bf16)
    dkv[:, 1] = dv[...].astype(bf16)
    for s in range(SLOTS):
        for l in range(2):
            lanes = pl.ds(l * HEAD_SIZE, HEAD_SIZE)
            part = (dq[2 * s + l] * scale).T
            if s % 2 == 0:
                keep[s // 2, :, lanes] = part
            else:
                send[s // 2, :, lanes] = part.astype(bf16)


def attention(mask, kv, xs):
    vmem = pl.BlockSpec(memory_space=pltpu.VMEM)
    rows = (SLAB_QUERIES, 2 * HEAD_SIZE)
    return pl.pallas_call(
        attention_kernel,
        out_shape=(
            jax.ShapeDtypeStruct((Z, 2, HALF, HEAD_SIZE), bf16),
            jax.ShapeDtypeStruct((2, *rows), f32),
            jax.ShapeDtypeStruct((2, *rows), bf16),
        ),
        in_specs=[pl.BlockSpec(memory_space=pltpu.SMEM)] + [vmem] * 5,
        out_specs=(vmem, vmem, vmem),
        scratch_shapes=[
            pltpu.SMEM((2 * Z,), jnp.int32),
            pltpu.VMEM((2 * SLOTS, SLAB_QUERIES, HEAD_SIZE), bf16),
            pltpu.VMEM((2 * SLOTS, SLAB_QUERIES, HEAD_SIZE), bf16),
            pltpu.VMEM((2 * SLOTS, 1, SLAB_QUERIES), f32),
            pltpu.VMEM((2 * SLOTS, 1, SLAB_QUERIES), f32),
            pltpu.VMEM((PICK * HALF, HEAD_SIZE), bf16),
            pltpu.VMEM((PICK * HALF, HEAD_SIZE), bf16),
            pltpu.VMEM((Z, HALF, HEAD_SIZE), f32),
            pltpu.VMEM((Z, HALF, HEAD_SIZE), f32),
            pltpu.VMEM((2 * SLOTS, HEAD_SIZE, SLAB_QUERIES), f32),
        ],
        compiler_params=pltpu.CompilerParams(vmem_limit_bytes=20 * 2**20),
        cost_estimate=pl.CostEstimate(
            flops=5 * 2 * 4096 * 1024 * 128 // 3,
            bytes_accessed=6 * 2**20,
            transcendentals=4096 * 1024 // 3,
        ),
        name="attention",
    )(mask, kv, *xs)


def other_core(value):
    return lax.ppermute(value, "core", [(0, 1), (1, 0)])


def other_chip(value):
    return lax.ppermute(value, "z", [(z, z ^ 1) for z in range(Z)])


def compute(queries, keys, values, forward_output, output_gradient, log_sum_norm, block_attend_mask):
    core, y, x = (lax.axis_index(axis) for axis in ("core", "y", "x"))
    own_kv, x0 = prepare(
        jnp.full((1,), y * X + x, jnp.int32), queries, keys, values, forward_output, output_gradient,
        log_sum_norm, block_attend_mask,
    )
    x2 = other_chip(x0)
    kv = lax.all_to_all(own_kv, "z", 0, 0, tiled=True)
    x1 = other_core(x0)
    x3 = other_core(x2)
    slots = (x0, x1, x2, x3)
    at = 2 * SLAB_QUERIES + 16
    mask = jnp.concatenate(
        [lax.dynamic_slice_in_dim(a[at:at + 8], core * Z, Z, 1) for a in slots]
    ).astype(jnp.int32)

    dkv, keep, send = attention(mask, kv, slots)

    got = other_core(send)
    back = lax.all_to_all(dkv, "z", 0, 0, tiled=True)
    own, *sent = reduce_step(to_row_kernel, jnp.full((1,), x, jnp.int32), (2, Y, TILE, 2 * HEAD_SIZE), keep, got)
    gots = [around(a, "x", d + 1) for d, a in enumerate(sent)]
    own, *sent = reduce_step(to_tile_kernel, jnp.full((1,), y, jnp.int32), (2, TILE, 2 * HEAD_SIZE), own, *gots)
    gots = [around(a, "y", d + 1) for d, a in enumerate(sent)]
    total = own + sum(a.astype(f32) for a in gots)
    other = other_chip(total[1].astype(bf16))
    grad_queries = (total[0] + other.astype(f32)).astype(bf16)

    def in_place(array):
        halves = array.reshape(KEY_VALUE_HEADS, 2, HALF, HEAD_SIZE)
        return halves.transpose(1, 2, 0, 3).reshape(BLK, KEY_VALUE_HEADS * HEAD_SIZE)

    return grad_queries, in_place(back[:, 0]), in_place(back[:, 1])


def solution(mesh):
    fine = Mesh(mesh.devices.reshape(Z, CORES, Y, X), ("z", "core", "y", "x"))
    ctx, rep = ("z", "core"), ("y", "x")
    in_specs = (
        P(None, ctx),
        P((*ctx, *rep), None),
        P((*ctx, *rep), None),
        P(None, ctx),
        P(None, ctx),
        P(ctx, None),
        P(ctx, None, None),
    )
    out_specs = (P(rep, ctx), P((*ctx, *rep), None), P((*ctx, *rep), None))
    return jax.shard_map(compute, mesh=fine, in_specs=in_specs, out_specs=out_specs, check_vma=False)
```

time: 273 us -> 128 us (0.47)
  the two profiles are of different devices: /device:TPU:1 before, /device:TPU:56 now
where the time goes in v1:
time: 128 us; the launch traced here: 127 us
  starting transfers between devices  57.4 us (45%)
  waiting for transfers between devices  46.9 us (37%)
  Pallas kernels  10.9 us (9%)
  local copies, waits for them, and re-layouts  10.4 us (8%)
    ppermute x2, waiting for transfers between devices, other_chip(): return lax.ppermute(value, 'z', [(z, z ^ 1) for z in range(Z)])  34.3 us
    ppermute x6, starting transfers between devices, around(): lax.ppermute(value, axis, [(i, (i + distance) % 4) for i in range(4)])  20.9 us
    all_to_all x1, starting transfers between devices, compute(): kv = lax.all_to_all(own_kv, 'z', 0, 0, tiled=True)  15.2 us
    all_to_all x1, starting transfers between devices, compute(): back = lax.all_to_all(dkv, 'z', 0, 0, tiled=True)  11.5 us
    pallas_call x1, Pallas kernels, attention(): pl.pallas_call(attention_kernel, out_shape=(jax.ShapeDtypeStruct((Z, 2, H...  9.75 us
    ppermute x6, waiting for transfers between devices, around(): lax.ppermute(value, axis, [(i, (i + distance) % 4) for i in range(4)])  9.07 us
    unnamed x22, local copies, waits for them, and re-layouts  8.81 us
    ppermute x3, starting transfers between devices, other_core(): return lax.ppermute(value, 'core', [(0, 1), (1, 0)])  5.75 us
  transfers between devices with their start and end apart: 13, of which 8 were waited for; matrix products, arithmetic and copies ran while one was open for 1% of the time, Pallas kernels for 0%

profile of v1, /device:TPU:56, one launch (start us, length us, event | category | flops | bytes accessed | tf_op | source)
XLA Modules:
  0.0 127.1 jit_solution(14701003563346700495)
XLA Ops:
  0.7 0.7 copy-done.5
  1.4 0.9 copy-done
  2.3 0.9 copy-done.1
  3.3 0.9 copy-done.2
  4.2 0.9 copy-done.3
  5.2 0.9 copy-done.4
  6.1 0.7 copy-done.6
  6.8 1.0 prepare.1
  7.8 15.2 %all-to-all-start = ((bf16[16,2,64,128]{3,2,1,0:T(8,128)(2,1)}), bf16[16,2,64,128]{3,2,1,0:T(8,128)(2,1)S(1)}, u32[]{:S(2)}, u32[]{:S(2)}) async-start(bf16[16,2,64,128]{3,2,1,0:T(8,128)(2,1)} %get-tuple-element.17), calls=%async_computation | async-start | bytes 1048576 | tf_op jit(solution)/shard_map/all_to_all | solution.py:234
  23.1 2.0 %collective-permute-start.1 = (bf16[1056,256]{1,0:T(8,128)(2,1)S(1)}, bf16[1056,256]{1,0:T(8,128)(2,1)S(1)}, u32[]{:S(2)}, u32[]{:S(2)}) collective-permute-start(bf16[1056,256]{1,0:T(8,128)(2,1)S(1)} %get-tuple-element.16.x0), channel_id=1, source_target_pairs={{0,32},{32,0},{64,96},{96,64},{128,160},{160,128},{192,224},{224,1... | collective-permute-start | bytes 1622024 | tf_op jit(solution)/shard_map/ppermute | solution.py:224
  25.1 1.9 %collective-permute-start = (bf16[1056,256]{1,0:T(8,128)(2,1)S(1)}, bf16[1056,256]{1,0:T(8,128)(2,1)S(1)}, u32[]{:S(2)}, u32[]{:S(2)}) collective-permute-start(bf16[1056,256]{1,0:T(8,128)(2,1)S(1)} %get-tuple-element.16.x0), channel_id=1, source_target_pairs={{0,16},{16,0},{1,17},{17,1},{2,18},{18,2},{3,19},{19,3},{4,20},{20... | collective-permute-start | bytes 1622024 | tf_op jit(solution)/shard_map/ppermute | solution.py:220
  27.0 30.7 %collective-permute-done.1.x2 = bf16[1056,256]{1,0:T(8,128)(2,1)S(1)} collective-permute-done((bf16[1056,256]{1,0:T(8,128)(2,1)S(1)}, bf16[1056,256]{1,0:T(8,128)(2,1)S(1)}, u32[]{:S(2)}, u32[]{:S(2)}) %collective-permute-start.1) | collective-permute-done | bytes 540704 | tf_op jit(solution)/shard_map/ppermute | solution.py:224
  57.7 1.9 %collective-permute-start.2 = (bf16[1056,256]{1,0:T(8,128)(2,1)S(1)}, bf16[1056,256]{1,0:T(8,128)(2,1)S(1)}, u32[]{:S(2)}, u32[]{:S(2)}) collective-permute-start(bf16[1056,256]{1,0:T(8,128)(2,1)S(1)} %collective-permute-done.1.x2), channel_id=1, source_target_pairs={{0,16},{16,0},{1,17},{17,1},{2,18},{18,2},{3,19},{19,3},{4,20},{20... | collective-permute-start | bytes 1622024 | tf_op jit(solution)/shard_map/ppermute | solution.py:220
  59.7 0.1 constant_dynamic-slice_fusion.3
  59.7 0.0 collective-permute-done.x1
  59.7 0.1 constant_dynamic-slice_fusion.1
  59.8 0.1 constant_dynamic-slice_fusion.2
  59.9 1.6 %collective-permute-done.2.x3 = bf16[1056,256]{1,0:T(8,128)(2,1)S(1)} collective-permute-done((bf16[1056,256]{1,0:T(8,128)(2,1)S(1)}, bf16[1056,256]{1,0:T(8,128)(2,1)S(1)}, u32[]{:S(2)}, u32[]{:S(2)}) %collective-permute-start.2) | collective-permute-done | bytes 540704 | tf_op jit(solution)/shard_map/ppermute | solution.py:220
  61.5 0.8 copy-done.7
  62.4 0.1 constant_dynamic-slice_fusion
  62.4 0.0 all-to-all-done.kv
  62.5 1.0 copy-done.8
  63.5 9.8 %attention.1 = (bf16[16,2,64,128]{3,2,1,0:T(8,128)(2,1)}, f32[2,512,256]{2,1,0:T(8,128)S(1)}, bf16[2,512,256]{2,1,0:T(8,128)(2,1)S(1)}) custom-call(s32[32,16]{1,0:T(8,128)S(1)} %maximum_convert_fusion.mask, bf16[16,2,64,128]{3,2,1,0:T(8,128)(2,1)S(1)} %all-to-all-done.kv, bf16[1056,256]{1,0:T(8,128)(2,1)S(1)} %get-tuple-element.16.x0, ...), custom_call_target="tpu_custom_call" | custom-call | flops 1789569664 | bytes 6291456 | tf_op jit(solution)/shard_map/attention/pallas_call | solution.py:188
  73.2 0.8 copy-done.9
  74.1 11.5 %all-to-all-start.1 = ((bf16[16,2,64,128]{3,2,1,0:T(8,128)(2,1)}), bf16[16,2,64,128]{3,2,1,0:T(8,128)(2,1)S(1)}, u32[]{:S(2)}, u32[]{:S(2)}) async-start(bf16[16,2,64,128]{3,2,1,0:T(8,128)(2,1)} %get-tuple-element.28), calls=%async_computation.1 | async-start | bytes 1048576 | tf_op jit(solution)/shard_map/all_to_all | solution.py:246
  85.6 1.9 %collective-permute-start.3 = (bf16[2,512,256]{2,1,0:T(8,128)(2,1)S(1)}, bf16[2,512,256]{2,1,0:T(8,128)(2,1)S(1)}, u32[]{:S(2)}, u32[]{:S(2)}) collective-permute-start(bf16[2,512,256]{2,1,0:T(8,128)(2,1)S(1)} %copy-done.10), channel_id=1, source_target_pairs={{0,16},{16,0},{1,17},{17,1},{2,18},{18,2},{3,19},{19,3},{4,20},{20... | collective-permute-start | bytes 1572872 | tf_op jit(solution)/shard_map/ppermute | solution.py:220
  87.5 1.9 %collective-permute-done.3.got = bf16[2,512,256]{2,1,0:T(8,128)(2,1)S(1)} collective-permute-done((bf16[2,512,256]{2,1,0:T(8,128)(2,1)S(1)}, bf16[2,512,256]{2,1,0:T(8,128)(2,1)S(1)}, u32[]{:S(2)}, u32[]{:S(2)}) %collective-permute-start.3) | collective-permute-done | bytes 524320 | tf_op jit(solution)/shard_map/ppermute | solution.py:220
  89.4 0.1 shard_map.94
  89.5 4.8 %collective-permute-start.4 = (bf16[2,4,32,256]{3,2,1,0:T(8,128)(2,1)S(1)}, bf16[2,4,32,256]{3,2,1,0:T(8,128)(2,1)S(1)}, u32[]{:S(2)}, u32[]{:S(2)}) collective-permute-start(bf16[2,4,32,256]{3,2,1,0:T(8,128)(2,1)S(1)} %get-tuple-element.21), channel_id=1, source_target_pairs={{0,1},{1,2},{2,3},{3,0},{4,5},{5,6},{6,7},{7,4},{8,9},{9,10},{10,1... | collective-permute-start | bytes 393224 | tf_op jit(solution)/shard_map/ppermute | solution.py:106
  94.3 3.7 %collective-permute-start.5 = (bf16[2,4,32,256]{3,2,1,0:T(8,128)(2,1)S(1)}, bf16[2,4,32,256]{3,2,1,0:T(8,128)(2,1)S(1)}, u32[]{:S(2)}, u32[]{:S(2)}) collective-permute-start(bf16[2,4,32,256]{3,2,1,0:T(8,128)(2,1)S(1)} %get-tuple-element.22), channel_id=1, source_target_pairs={{0,2},{1,3},{2,0},{3,1},{4,6},{5,7},{6,4},{7,5},{8,10},{9,11},{10,... | collective-permute-start | bytes 393224 | tf_op jit(solution)/shard_map/ppermute | solution.py:106
  98.0 2.9 %collective-permute-start.6 = (bf16[2,4,32,256]{3,2,1,0:T(8,128)(2,1)S(1)}, bf16[2,4,32,256]{3,2,1,0:T(8,128)(2,1)S(1)}, u32[]{:S(2)}, u32[]{:S(2)}) collective-permute-start(bf16[2,4,32,256]{3,2,1,0:T(8,128)(2,1)S(1)} %get-tuple-element.23), channel_id=1, source_target_pairs={{0,3},{1,0},{2,1},{3,2},{4,7},{5,4},{6,5},{7,6},{8,11},{9,8},{10,9... | collective-permute-start | bytes 393224 | tf_op jit(solution)/shard_map/ppermute | solution.py:106
  100.9 0.0 collective-permute-done.4.got1
  100.9 2.1 %collective-permute-done.5.got2 = bf16[2,4,32,256]{3,2,1,0:T(8,128)(2,1)S(1)} collective-permute-done((bf16[2,4,32,256]{3,2,1,0:T(8,128)(2,1)S(1)}, bf16[2,4,32,256]{3,2,1,0:T(8,128)(2,1)S(1)}, u32[]{:S(2)}, u32[]{:S(2)}) %collective-permute-start.5) | collective-permute-done | bytes 131104 | tf_op jit(solution)/shard_map/ppermute | solution.py:106
  102.9 1.9 %collective-permute-done.6.got3 = bf16[2,4,32,256]{3,2,1,0:T(8,128)(2,1)S(1)} collective-permute-done((bf16[2,4,32,256]{3,2,1,0:T(8,128)(2,1)S(1)}, bf16[2,4,32,256]{3,2,1,0:T(8,128)(2,1)S(1)}, u32[]{:S(2)}, u32[]{:S(2)}) %collective-permute-start.6) | collective-permute-done | bytes 131104 | tf_op jit(solution)/shard_map/ppermute | solution.py:106
  104.9 0.1 shard_map.95
  104.9 3.1 %collective-permute-start.7 = (bf16[2,32,256]{2,1,0:T(8,128)(2,1)S(1)}, bf16[2,32,256]{2,1,0:T(8,128)(2,1)S(1)}, u32[]{:S(2)}, u32[]{:S(2)}) collective-permute-start(bf16[2,32,256]{2,1,0:T(8,128)(2,1)S(1)} %get-tuple-element.25), channel_id=1, source_target_pairs={{0,4},{4,8},{8,12},{12,0},{1,5},{5,9},{9,13},{13,1},{2,6},{6,10},{... | collective-permute-start | bytes 98312 | tf_op jit(solution)/shard_map/ppermute | solution.py:106
  108.0 4.5 %collective-permute-start.8 = (bf16[2,32,256]{2,1,0:T(8,128)(2,1)S(1)}, bf16[2,32,256]{2,1,0:T(8,128)(2,1)S(1)}, u32[]{:S(2)}, u32[]{:S(2)}) collective-permute-start(bf16[2,32,256]{2,1,0:T(8,128)(2,1)S(1)} %get-tuple-element.26), channel_id=1, source_target_pairs={{0,8},{4,12},{8,0},{12,4},{1,9},{5,13},{9,1},{13,5},{2,10},{6,14},... | collective-permute-start | bytes 98312 | tf_op jit(solution)/shard_map/ppermute | solution.py:106
  112.5 1.9 %collective-permute-start.9 = (bf16[2,32,256]{2,1,0:T(8,128)(2,1)S(1)}, bf16[2,32,256]{2,1,0:T(8,128)(2,1)S(1)}, u32[]{:S(2)}, u32[]{:S(2)}) collective-permute-start(bf16[2,32,256]{2,1,0:T(8,128)(2,1)S(1)} %get-tuple-element.27), channel_id=1, source_target_pairs={{0,12},{4,0},{8,4},{12,8},{1,13},{5,1},{9,5},{13,9},{2,14},{6,2},{... | collective-permute-start | bytes 98312 | tf_op jit(solution)/shard_map/ppermute | solution.py:106
  114.4 0.0 collective-permute-done.7
  114.4 0.9 collective-permute-done.8
  115.3 4.2 %collective-permute-done.9 = bf16[2,32,256]{2,1,0:T(8,128)(2,1)S(1)} collective-permute-done((bf16[2,32,256]{2,1,0:T(8,128)(2,1)S(1)}, bf16[2,32,256]{2,1,0:T(8,128)(2,1)S(1)}, u32[]{:S(2)}, u32[]{:S(2)}) %collective-permute-start.9) | collective-permute-done | bytes 32800 | tf_op jit(solution)/shard_map/ppermute | solution.py:106
  119.6 2.0 %collective-permute-start.10 = (bf16[32,256]{1,0:T(8,128)(2,1)S(1)}, bf16[32,256]{1,0:T(8,128)(2,1)S(1)}, u32[]{:S(2)}, u32[]{:S(2)}) collective-permute-start(bf16[32,256]{1,0:T(8,128)(2,1)S(1)} %fusion.2), channel_id=1, source_target_pairs={{0,32},{32,0},{64,96},{96,64},{128,160},{160,128},{192,224},{224,1... | collective-permute-start | bytes 49160 | tf_op jit(solution)/shard_map/ppermute | solution.py:224
  121.6 3.6 %collective-permute-done.10 = bf16[32,256]{1,0:T(8,128)(2,1)S(1)} collective-permute-done((bf16[32,256]{1,0:T(8,128)(2,1)S(1)}, bf16[32,256]{1,0:T(8,128)(2,1)S(1)}, u32[]{:S(2)}, u32[]{:S(2)}) %collective-permute-start.10) | collective-permute-done | bytes 16416 | tf_op jit(solution)/shard_map/ppermute | solution.py:224
  125.2 0.6 fusion.1
  125.8 0.0 all-to-all-done.1
  125.8 0.2 copy.11
  126.0 0.2 copy.10
  126.2 0.9 copy_bitcast_fusion
  (20 shorter events, 0.1 us)
Async XLA Ops:
  0.6 0.7 copy-start.5
  1.4 0.9 copy-start
  2.3 0.9 copy-start.1
  3.3 0.9 copy-start.2
  4.2 0.9 copy-start.3
  5.2 0.9 copy-start.4
  6.1 0.7 copy-start.6
  7.8 54.6 %all-to-all-start = ((bf16[16,2,64,128]{3,2,1,0:T(8,128)(2,1)}), bf16[16,2,64,128]{3,2,1,0:T(8,128)(2,1)S(1)}, u32[]{:S(2)}, u32[]{:S(2)}) async-start(bf16[16,2,64,128]{3,2,1,0:T(8,128)(2,1)} %get-tuple-element.17), calls=%async_computation | async-start | bytes 1048576 | tf_op jit(solution)/shard_map/all_to_all | solution.py:234
  23.1 34.7 %collective-permute-start.1 = (bf16[1056,256]{1,0:T(8,128)(2,1)S(1)}, bf16[1056,256]{1,0:T(8,128)(2,1)S(1)}, u32[]{:S(2)}, u32[]{:S(2)}) collective-permute-start(bf16[1056,256]{1,0:T(8,128)(2,1)S(1)} %get-tuple-element.16.x0), channel_id=1, source_target_pairs={{0,32},{32,0},{64,96},{96,64},{128,160},{160,128},{192,224},{224,1... | collective-permute-start | bytes 1622024 | tf_op jit(solution)/shard_map/ppermute | solution.py:224
  25.1 34.7 %collective-permute-start = (bf16[1056,256]{1,0:T(8,128)(2,1)S(1)}, bf16[1056,256]{1,0:T(8,128)(2,1)S(1)}, u32[]{:S(2)}, u32[]{:S(2)}) collective-permute-start(bf16[1056,256]{1,0:T(8,128)(2,1)S(1)} %get-tuple-element.16.x0), channel_id=1, source_target_pairs={{0,16},{16,0},{1,17},{17,1},{2,18},{18,2},{3,19},{19,3},{4,20},{20... | collective-permute-start | bytes 1622024 | tf_op jit(solution)/shard_map/ppermute | solution.py:220
  57.7 3.8 %collective-permute-start.2 = (bf16[1056,256]{1,0:T(8,128)(2,1)S(1)}, bf16[1056,256]{1,0:T(8,128)(2,1)S(1)}, u32[]{:S(2)}, u32[]{:S(2)}) collective-permute-start(bf16[1056,256]{1,0:T(8,128)(2,1)S(1)} %collective-permute-done.1.x2), channel_id=1, source_target_pairs={{0,16},{16,0},{1,17},{17,1},{2,18},{18,2},{3,19},{19,3},{4,20},{20... | collective-permute-start | bytes 1622024 | tf_op jit(solution)/shard_map/ppermute | solution.py:220
  61.5 0.8 copy-start.7
  62.4 1.0 copy-start.8
  73.2 0.8 copy-start.9
  74.1 11.5 %copy-start.10 = (bf16[2,512,256]{2,1,0:T(8,128)(2,1)S(1)}, bf16[2,512,256]{2,1,0:T(8,128)(2,1)}, u32[]{:S(2)}) copy-start(bf16[2,512,256]{2,1,0:T(8,128)(2,1)} %copy-done.9) | copy-start | bytes 1572868
  74.1 51.7 %all-to-all-start.1 = ((bf16[16,2,64,128]{3,2,1,0:T(8,128)(2,1)}), bf16[16,2,64,128]{3,2,1,0:T(8,128)(2,1)S(1)}, u32[]{:S(2)}, u32[]{:S(2)}) async-start(bf16[16,2,64,128]{3,2,1,0:T(8,128)(2,1)} %get-tuple-element.28), calls=%async_computation.1 | async-start | bytes 1048576 | tf_op jit(solution)/shard_map/all_to_all | solution.py:246
  85.6 3.8 %collective-permute-start.3 = (bf16[2,512,256]{2,1,0:T(8,128)(2,1)S(1)}, bf16[2,512,256]{2,1,0:T(8,128)(2,1)S(1)}, u32[]{:S(2)}, u32[]{:S(2)}) collective-permute-start(bf16[2,512,256]{2,1,0:T(8,128)(2,1)S(1)} %copy-done.10), channel_id=1, source_target_pairs={{0,16},{16,0},{1,17},{17,1},{2,18},{18,2},{3,19},{19,3},{4,20},{20... | collective-permute-start | bytes 1572872 | tf_op jit(solution)/shard_map/ppermute | solution.py:220
  89.5 11.4 %collective-permute-start.4 = (bf16[2,4,32,256]{3,2,1,0:T(8,128)(2,1)S(1)}, bf16[2,4,32,256]{3,2,1,0:T(8,128)(2,1)S(1)}, u32[]{:S(2)}, u32[]{:S(2)}) collective-permute-start(bf16[2,4,32,256]{3,2,1,0:T(8,128)(2,1)S(1)} %get-tuple-element.21), channel_id=1, source_target_pairs={{0,1},{1,2},{2,3},{3,0},{4,5},{5,6},{6,7},{7,4},{8,9},{9,10},{10,1... | collective-permute-start | bytes 393224 | tf_op jit(solution)/shard_map/ppermute | solution.py:106
  94.3 8.7 %collective-permute-start.5 = (bf16[2,4,32,256]{3,2,1,0:T(8,128)(2,1)S(1)}, bf16[2,4,32,256]{3,2,1,0:T(8,128)(2,1)S(1)}, u32[]{:S(2)}, u32[]{:S(2)}) collective-permute-start(bf16[2,4,32,256]{3,2,1,0:T(8,128)(2,1)S(1)} %get-tuple-element.22), channel_id=1, source_target_pairs={{0,2},{1,3},{2,0},{3,1},{4,6},{5,7},{6,4},{7,5},{8,10},{9,11},{10,... | collective-permute-start | bytes 393224 | tf_op jit(solution)/shard_map/ppermute | solution.py:106
  98.0 6.9 %collective-permute-start.6 = (bf16[2,4,32,256]{3,2,1,0:T(8,128)(2,1)S(1)}, bf16[2,4,32,256]{3,2,1,0:T(8,128)(2,1)S(1)}, u32[]{:S(2)}, u32[]{:S(2)}) collective-permute-start(bf16[2,4,32,256]{3,2,1,0:T(8,128)(2,1)S(1)} %get-tuple-element.23), channel_id=1, source_target_pairs={{0,3},{1,0},{2,1},{3,2},{4,7},{5,4},{6,5},{7,6},{8,11},{9,8},{10,9... | collective-permute-start | bytes 393224 | tf_op jit(solution)/shard_map/ppermute | solution.py:106
  104.9 9.5 %collective-permute-start.7 = (bf16[2,32,256]{2,1,0:T(8,128)(2,1)S(1)}, bf16[2,32,256]{2,1,0:T(8,128)(2,1)S(1)}, u32[]{:S(2)}, u32[]{:S(2)}) collective-permute-start(bf16[2,32,256]{2,1,0:T(8,128)(2,1)S(1)} %get-tuple-element.25), channel_id=1, source_target_pairs={{0,4},{4,8},{8,12},{12,0},{1,5},{5,9},{9,13},{13,1},{2,6},{6,10},{... | collective-permute-start | bytes 98312 | tf_op jit(solution)/shard_map/ppermute | solution.py:106
  108.0 7.3 %collective-permute-start.8 = (bf16[2,32,256]{2,1,0:T(8,128)(2,1)S(1)}, bf16[2,32,256]{2,1,0:T(8,128)(2,1)S(1)}, u32[]{:S(2)}, u32[]{:S(2)}) collective-permute-start(bf16[2,32,256]{2,1,0:T(8,128)(2,1)S(1)} %get-tuple-element.26), channel_id=1, source_target_pairs={{0,8},{4,12},{8,0},{12,4},{1,9},{5,13},{9,1},{13,5},{2,10},{6,14},... | collective-permute-start | bytes 98312 | tf_op jit(solution)/shard_map/ppermute | solution.py:106
  112.5 7.0 %collective-permute-start.9 = (bf16[2,32,256]{2,1,0:T(8,128)(2,1)S(1)}, bf16[2,32,256]{2,1,0:T(8,128)(2,1)S(1)}, u32[]{:S(2)}, u32[]{:S(2)}) collective-permute-start(bf16[2,32,256]{2,1,0:T(8,128)(2,1)S(1)} %get-tuple-element.27), channel_id=1, source_target_pairs={{0,12},{4,0},{8,4},{12,8},{1,13},{5,1},{9,5},{13,9},{2,14},{6,2},{... | collective-permute-start | bytes 98312 | tf_op jit(solution)/shard_map/ppermute | solution.py:106
  119.6 5.6 %collective-permute-start.10 = (bf16[32,256]{1,0:T(8,128)(2,1)S(1)}, bf16[32,256]{1,0:T(8,128)(2,1)S(1)}, u32[]{:S(2)}, u32[]{:S(2)}) collective-permute-start(bf16[32,256]{1,0:T(8,128)(2,1)S(1)} %fusion.2), channel_id=1, source_target_pairs={{0,32},{32,0},{64,96},{96,64},{128,160},{160,128},{192,224},{224,1... | collective-permute-start | bytes 49160 | tf_op jit(solution)/shard_map/ppermute | solution.py:224

commit v2 on v1

v2 whole, which is shorter than its diff:
```python
import math

import jax
import jax.numpy as jnp
from jax import lax
from jax.experimental import pallas as pl
from jax.experimental.pallas import tpu as pltpu
from jax.sharding import Mesh, PartitionSpec as P


KEY_VALUE_HEADS = 8
HEAD_SIZE = 128
BLK = 128
SLAB_QUERIES = 512
Z, CORES, Y, X = 16, 2, 4, 4
SLOTS = 4
HALF = BLK // 2
TILE = SLAB_QUERIES // (Y * X)
AUX = 32
PACKED = 2 * SLAB_QUERIES + AUX
PICK = 4
LOG2E = math.log2(math.e)
NEVER = -1e30
f32, bf16 = jnp.float32, jnp.bfloat16


def dot(a, b, dims):
    return lax.dot_general(a, b, (dims, ((), ())), preferred_element_type=f32)


def prepare_kernel(rep, queries, keys, values, output, cotangent, norm, mask, kv, packed,
                   out_buf, norm_buf, mask_buf, sems):
    copies = [
        pltpu.make_async_copy(source, target, sems.at[i])
        for i, (source, target) in enumerate(
            (
                (cotangent, packed.at[pl.ds(SLAB_QUERIES, SLAB_QUERIES)]),
                (output, out_buf),
                (mask, mask_buf),
                (norm, norm_buf),
                (queries, packed.at[pl.ds(0, SLAB_QUERIES)]),
            )
        )
    ]
    for i, source in enumerate((keys, values)):
        for g in range(KEY_VALUE_HEADS):
            for half in range(2):
                part = source.at[pl.ds(half * HALF, HALF), pl.ds(g * HEAD_SIZE, HEAD_SIZE)]
                t = 2 * g + half
                copies.append(pltpu.make_async_copy(part, kv.at[t, i], sems.at[5 + 2 * t + i]))
    for copy in copies:
        copy.start()
    block = lax.broadcasted_iota(jnp.int32, (CORES * Z * Y * X, HEAD_SIZE), 0)
    lane = lax.broadcasted_iota(jnp.int32, (CORES * Z * Y * X, HEAD_SIZE), 1)
    wanted = ((lane % Z) * CORES + lane // Z) * (Y * X) + rep[0]
    pick = jnp.where((block == wanted) & (lane < CORES * Z), 1.0, 0.0).astype(bf16)
    for copy in copies[:4]:
        copy.wait()
    rows = []
    for l in range(2):
        lanes = slice(l * HEAD_SIZE, (l + 1) * HEAD_SIZE)
        own = packed[SLAB_QUERIES:2 * SLAB_QUERIES, lanes]
        product = own.astype(f32) * out_buf[:, lanes].astype(f32)
        rows.append(jnp.sum(product.T, axis=0, keepdims=True))
    rows += [norm_buf[l:l + 1] * (-LOG2E) for l in range(2)]
    wide = 2 * HEAD_SIZE
    exact = jnp.concatenate([r[:, i * wide:(i + 1) * wide] for r in rows for i in range(2)], axis=0)
    high = exact.astype(bf16).astype(f32)
    attend = jnp.concatenate([mask_buf[0], mask_buf[1]], axis=0).astype(f32).astype(bf16)
    picked = dot(attend, pick, ((1,), (0,)))
    picked = jnp.concatenate([picked, jnp.zeros((8, HEAD_SIZE), f32)], axis=1)
    aux = jnp.concatenate([high, exact - high, picked, jnp.zeros((AUX - 24, wide), f32)], axis=0)
    packed[2 * SLAB_QUERIES:] = aux.astype(bf16)
    copies[4].wait()
    for copy in copies[5:]:
        copy.wait()


def prepare(rep, *arrays):
    vmem = pl.BlockSpec(memory_space=pltpu.VMEM)
    wide = 2 * HEAD_SIZE
    return pl.pallas_call(
        prepare_kernel,
        out_shape=(
            jax.ShapeDtypeStruct((Z, 2, HALF, HEAD_SIZE), bf16),
            jax.ShapeDtypeStruct((PACKED, wide), bf16),
        ),
        in_specs=[pl.BlockSpec(memory_space=pltpu.SMEM)] + [pl.BlockSpec(memory_space=pltpu.HBM)] * 7,
        out_specs=(vmem, vmem),
        scratch_shapes=[
            pltpu.VMEM((SLAB_QUERIES, wide), bf16),
            pltpu.VMEM((2, SLAB_QUERIES), f32),
            pltpu.VMEM((2, 4, CORES * Z * Y * X), jnp.int32),
            pltpu.SemaphoreType.DMA((5 + 4 * KEY_VALUE_HEADS,)),
        ],
        name="prepare",
    )(rep, *arrays)


def place_kernel(back, key_grad, value_grad):
    for g in range(KEY_VALUE_HEADS):
        for half in range(2):
            at = (slice(half * HALF, (half + 1) * HALF), slice(g * HEAD_SIZE, (g + 1) * HEAD_SIZE))
            key_grad[at] = back[2 * g + half, 0]
            value_grad[at] = back[2 * g + half, 1]


def placed(back):
    vmem = pl.BlockSpec(memory_space=pltpu.VMEM)
    return pl.pallas_call(
        place_kernel,
        out_shape=(jax.ShapeDtypeStruct((BLK, KEY_VALUE_HEADS * HEAD_SIZE), bf16),) * 2,
        in_specs=[vmem],
        out_specs=(vmem, vmem),
        compiler_params=pltpu.CompilerParams(vmem_limit_bytes=8 * 2**20),
        name="place",
    )(back)


def halve_kernel(bit, keep, got, own, sent):
    mine, other = bit[0], 1 - bit[0]
    for i in range(own.shape[0]):
        own[i] = keep[i, mine].astype(f32) + got[i, mine].astype(f32)
        sent[i] = (keep[i, other].astype(f32) + got[i, other].astype(f32)).astype(bf16)


def halve(bit, keep, got):
    count = keep.size // (2 * TILE * 2 * HEAD_SIZE)
    half = (count, TILE, 2 * HEAD_SIZE)
    whole = (count, 2, TILE, 2 * HEAD_SIZE)
    vmem = pl.BlockSpec(memory_space=pltpu.VMEM)
    return pl.pallas_call(
        halve_kernel,
        out_shape=(jax.ShapeDtypeStruct(half, f32), jax.ShapeDtypeStruct(half, bf16)),
        in_specs=[pl.BlockSpec(memory_space=pltpu.SMEM), vmem, vmem],
        out_specs=(vmem, vmem),
        compiler_params=pltpu.CompilerParams(vmem_limit_bytes=8 * 2**20),
        name="halve",
    )(jnp.full((1,), bit, jnp.int32), keep.reshape(whole), got.reshape(whole))


def across(value, axis, distance):
    return lax.ppermute(value, axis, [(i, i ^ distance) for i in range(4)])


def attention_kernel(mask, order, kv, x0, x1, x2, x3, dkv, keep, send,
                     xs, norm, dots, kbuf, vbuf, dk, dv, dq, sems):
    scale = HEAD_SIZE ** -0.5
    copies = [pltpu.make_async_copy(x, xs.at[s], sems.at[s]) for s, x in enumerate((x0, x1, x2, x3))]
    for copy in copies:
        copy.start()
    dk[...] = jnp.zeros_like(dk)
    dv[...] = jnp.zeros_like(dv)
    dq[...] = jnp.zeros_like(dq)

    def head(h, _):
        for s, copy in enumerate(copies):
            @pl.when(h == 2 * s)
            def _():
                copy.wait()
                aux = xs[s, 2 * SLAB_QUERIES:, :].astype(f32)
                aux = aux[:8] + aux[8:16]
                for l in range(2):
                    dots[2 * s + l] = jnp.concatenate([aux[2 * l:2 * l + 1], aux[2 * l + 1:2 * l + 2]], axis=1)
                    norm[2 * s + l] = jnp.concatenate([aux[2 * l + 4:2 * l + 5], aux[2 * l + 5:2 * l + 6]], axis=1)

        s, lanes = h // 2, pl.ds(pl.multiple_of((h % 2) * HEAD_SIZE, HEAD_SIZE), HEAD_SIZE)

        def turn(t, _):
            picked = [order[h, t * PICK + j] for j in range(PICK)]
            rows = []
            for j, i in enumerate(picked):
                kbuf[pl.ds(j * HALF, HALF), :] = kv[i, 0]
                vbuf[pl.ds(j * HALF, HALF), :] = kv[i, 1]
                row = jnp.concatenate(
                    [
                        jnp.where(mask[h * 4 + qb, i] > 0, norm[h, :, pl.ds(qb * BLK, BLK)], NEVER)
                        for qb in range(4)
                    ],
                    axis=1,
                )
                rows.append(jnp.broadcast_to(row, (HALF, SLAB_QUERIES)))
            bias = jnp.concatenate(rows, axis=0)
            q, g = xs[s, :SLAB_QUERIES, lanes], xs[s, SLAB_QUERIES:2 * SLAB_QUERIES, lanes]
            scores = dot(kbuf[...], q, ((1,), (1,)))
            w = jnp.exp2(scores * (scale * LOG2E) + bias)
            gw = dot(vbuf[...], g, ((1,), (1,)))
            ds = (w * (gw - dots[h])).astype(bf16)
            dv_part = dot(w.astype(bf16), g, ((1,), (0,)))
            dk_part = dot(ds, q, ((1,), (0,)))
            for j, i in enumerate(picked):
                dv[i] += dv_part[j * HALF:(j + 1) * HALF]
                dk[i] += dk_part[j * HALF:(j + 1) * HALF]
            dq[h] += dot(kbuf[...], ds, ((0,), (0,)))
            return 0

        lax.fori_loop(0, order[h, Z], turn, 0)
        return 0

    lax.fori_loop(0, 2 * SLOTS, head, 0)
    dkv[:, 0] = (dk[...] * scale).astype(bf16)
    dkv[:, 1] = dv[...].astype(bf16)
    for s in range(SLOTS):
        for l in range(2):
            lanes = pl.ds(l * HEAD_SIZE, HEAD_SIZE)
            part = (dq[2 * s + l] * scale).astype(bf16).T
            if s % 2 == 0:
                keep[s // 2, :, lanes] = part
            else:
                send[s // 2, :, lanes] = part


def attention(mask, order, kv, xs):
    vmem = pl.BlockSpec(memory_space=pltpu.VMEM)
    rows = (SLAB_QUERIES, 2 * HEAD_SIZE)
    return pl.pallas_call(
        attention_kernel,
        out_shape=(
            jax.ShapeDtypeStruct((Z, 2, HALF, HEAD_SIZE), bf16),
            jax.ShapeDtypeStruct((2, *rows), bf16),
            jax.ShapeDtypeStruct((2, *rows), bf16),
        ),
        in_specs=[pl.BlockSpec(memory_space=pltpu.SMEM)] * 2 + [vmem] + [pl.BlockSpec(memory_space=pl.ANY)] * 4,
        out_specs=(vmem, vmem, vmem),
        scratch_shapes=[
            pltpu.VMEM((SLOTS, PACKED, 2 * HEAD_SIZE), bf16),
            pltpu.VMEM((2 * SLOTS, 1, SLAB_QUERIES), f32),
            pltpu.VMEM((2 * SLOTS, 1, SLAB_QUERIES), f32),
            pltpu.VMEM((PICK * HALF, HEAD_SIZE), bf16),
            pltpu.VMEM((PICK * HALF, HEAD_SIZE), bf16),
            pltpu.VMEM((Z, HALF, HEAD_SIZE), f32),
            pltpu.VMEM((Z, HALF, HEAD_SIZE), f32),
            pltpu.VMEM((2 * SLOTS, HEAD_SIZE, SLAB_QUERIES), f32),
            pltpu.SemaphoreType.DMA((SLOTS,)),
        ],
        compiler_params=pltpu.CompilerParams(vmem_limit_bytes=28 * 2**20),
        cost_estimate=pl.CostEstimate(
            flops=5 * 2 * 4096 * 1024 * 128 // 3,
            bytes_accessed=6 * 2**20,
            transcendentals=4096 * 1024 // 3,
        ),
        name="attention",
    )(mask, order, kv, *xs)


def attended_first(mask):
    live = jnp.max(mask.reshape(2 * SLOTS, 4, Z), axis=1)
    index = jnp.arange(Z)
    earlier = (index[:, None] < index[None, :]).astype(jnp.int32)
    before = jnp.sum(live[:, :, None] * earlier, axis=1)
    count = jnp.sum(live, axis=1, keepdims=True)
    rank = jnp.where(live > 0, before, count + index[None, :] - before)
    order = jnp.sum(jnp.where(rank[:, :, None] == index, index[None, :, None], 0), axis=1)
    return jnp.concatenate([order, (count + PICK - 1) // PICK], axis=1).astype(jnp.int32)


def other_core(value):
    return lax.ppermute(value, "core", [(0, 1), (1, 0)])


def other_chip(value):
    return lax.ppermute(value, "z", [(z, z ^ 1) for z in range(Z)])


def compute(queries, keys, values, forward_output, output_gradient, log_sum_norm, block_attend_mask):
    core, y, x = (lax.axis_index(axis) for axis in ("core", "y", "x"))
    own_kv, x0 = prepare(
        jnp.full((1,), y * X + x, jnp.int32), queries, keys, values, forward_output, output_gradient,
        log_sum_norm, block_attend_mask,
    )
    x2 = other_chip(x0)
    kv = lax.all_to_all(own_kv, "z", 0, 0, tiled=True)
    x1 = other_core(x0)
    x3 = other_core(x2)
    slots = (x0, x1, x2, x3)
    at = 2 * SLAB_QUERIES + 16
    attended = [a[at:at + 8] for a in slots[:3]]
    attended.append(other_core(attended[2]))
    mask = jnp.concatenate(
        [lax.dynamic_slice_in_dim(a, core * Z, Z, 1) for a in attended]
    ).astype(jnp.int32)

    dkv, keep, send = attention(mask, attended_first(mask), kv, slots)

    got = other_core(send)
    own, sent = halve(x % 2, keep, got)
    got = across(sent, "x", 1)
    back = lax.all_to_all(dkv, "z", 0, 0, tiled=True)
    for bit, axis, distance in ((x // 2, "x", 2), (y % 2, "y", 1), (y // 2, "y", 2)):
        own, sent = halve(bit, own, got)
        got = across(sent, axis, distance)
    total = own + got.astype(f32)
    other = other_chip(total[1].astype(bf16))
    grad_queries = (total[0] + other.astype(f32)).astype(bf16)
    key_grad, value_grad = placed(back)
    return grad_queries, key_grad, value_grad


def solution(mesh):
    fine = Mesh(mesh.devices.reshape(Z, CORES, Y, X), ("z", "core", "y", "x"))
    ctx, rep = ("z", "core"), ("y", "x")
    in_specs = (
        P(None, ctx),
        P((*ctx, *rep), None),
        P((*ctx, *rep), None),
        P(None, ctx),
        P(None, ctx),
        P(ctx, None),
        P(ctx, None, None),
    )
    out_specs = (P(rep, ctx), P((*ctx, *rep), None), P((*ctx, *rep), None))
    return jax.shard_map(compute, mesh=fine, in_specs=in_specs, out_specs=out_specs, check_vma=False)
```

time: 128 us -> 115 us (0.90)
  the two profiles are of different devices: /device:TPU:56 before, /device:TPU:10 now
where the time goes in v2:
time: 115 us
  starting transfers between devices  49 us (43%)
  waiting for transfers between devices  47.9 us (42%)
  Pallas kernels  12.7 us (11%)
  local copies, waits for them, and re-layouts  3.05 us (3%)
    all_to_all x1, waiting for transfers between devices, compute(): kv = lax.all_to_all(own_kv, 'z', 0, 0, tiled=True)  22.2 us
    ppermute x4, waiting for transfers between devices, across(): return lax.ppermute(value, axis, [(i, i ^ distance) for i in range(4)])  21.1 us
    all_to_all x1, starting transfers between devices, compute(): kv = lax.all_to_all(own_kv, 'z', 0, 0, tiled=True)  14.3 us
    ppermute x4, starting transfers between devices, across(): return lax.ppermute(value, axis, [(i, i ^ distance) for i in range(4)])  11.1 us
    ppermute x4, starting transfers between devices, other_core(): return lax.ppermute(value, 'core', [(0, 1), (1, 0)])  9.24 us
    pallas_call x1, Pallas kernels, attention(): pl.pallas_call(attention_kernel, out_shape=(jax.ShapeDtypeStruct((Z, 2, H...  8.93 us
    ppermute x2, starting transfers between devices, other_chip(): return lax.ppermute(value, 'z', [(z, z ^ 1) for z in range(Z)])  7.51 us
    all_to_all x1, starting transfers between devices, compute(): back = lax.all_to_all(dkv, 'z', 0, 0, tiled=True)  6.8 us
  transfers between devices with their start and end apart: 12, of which 8 were waited for; matrix products, arithmetic and copies ran while one was open for 1% of the time, Pallas kernels for 0%

profile of v2, /device:TPU:10, one launch (start us, length us, event | category | flops | bytes accessed | tf_op | source)
XLA Modules:
  0.0 114.6 jit_solution(17049456782650488657)
XLA Ops:
  0.6 2.6 %prepare.1 = (bf16[16,2,64,128]{3,2,1,0:T(8,128)(2,1)}, bf16[1056,256]{1,0:T(8,128)(2,1)}) custom-call(s32[1]{0:T(128)} %bitcast.4.rep, bf16[512,256]{1,0:T(8,128)(2,1)} %queries.1, bf16[128,1024]{1,0:T(8,128)(2,1)} %keys.1, bf16[128,1024]{1,0:T(8,128)(2,1)} %values.1, bf16[512,256]{1,0:T(8,128)(2,1)} %output.1, bf16[512,256]{1,0:T(8,128)(2,1)} %cotangent.1, ...), custom_call_target="tpu_custom_call" | custom-call | tf_op jit(solution)/shard_map/prepare/pallas_call | solution.py:82
  3.3 0.0 copy-start
  3.3 4.0 %collective-permute-start.1 = (bf16[1056,256]{1,0:T(8,128)(2,1)}, bf16[1056,256]{1,0:T(8,128)(2,1)S(1)}, u32[]{:S(2)}, u32[]{:S(2)}) collective-permute-start(bf16[1056,256]{1,0:T(8,128)(2,1)} %get-tuple-element.18.x0), channel_id=1, source_target_pairs={{0,32},{32,0},{64,96},{96,64},{128,160},{160,128},{192,224},{224,1... | collective-permute-start | bytes 1622024 | tf_op jit(solution)/shard_map/ppermute | solution.py:262
  7.2 1.9 %collective-permute-start = (bf16[1056,256]{1,0:T(8,128)(2,1)}, bf16[1056,256]{1,0:T(8,128)(2,1)S(1)}, u32[]{:S(2)}, u32[]{:S(2)}) collective-permute-start(bf16[1056,256]{1,0:T(8,128)(2,1)} %get-tuple-element.18.x0), channel_id=1, source_target_pairs={{0,16},{16,0},{1,17},{17,1},{2,18},{18,2},{3,19},{19,3},{4,20},{20... | collective-permute-start | bytes 1622024 | tf_op jit(solution)/shard_map/ppermute | solution.py:258
  9.2 14.3 %all-to-all-start = ((bf16[16,2,64,128]{3,2,1,0:T(8,128)(2,1)}), bf16[16,2,64,128]{3,2,1,0:T(8,128)(2,1)S(1)}, u32[]{:S(2)}, u32[]{:S(2)}) async-start(bf16[16,2,64,128]{3,2,1,0:T(8,128)(2,1)} %get-tuple-element.19), calls=%async_computation | async-start | bytes 1048576 | tf_op jit(solution)/shard_map/all_to_all | solution.py:272
  23.5 0.0 copy-done
  23.5 0.1 constant_dynamic-slice_fusion.3
  23.6 0.0 collective-permute-done.1.x2
  23.6 2.1 %collective-permute-start.2 = (bf16[8,256]{1,0:T(8,128)(2,1)S(1)}, bf16[8,256]{1,0:T(8,128)(2,1)S(1)}, u32[]{:S(2)}, u32[]{:S(2)}) collective-permute-start(bf16[8,256]{1,0:T(8,128)(2,1)S(1)} %slice.22), channel_id=1, source_target_pairs={{0,16},{16,0},{1,17},{17,1},{2,18},{18,2},{3,19},{19,3},{4,20},{20... | collective-permute-start | bytes 12296 | tf_op jit(solution)/shard_map/ppermute | solution.py:258
  25.7 0.0 collective-permute-done.x1
  25.8 0.1 constant_dynamic-slice_fusion.1
  25.8 0.1 constant_dynamic-slice_fusion.2
  25.9 2.2 %collective-permute-start.3 = (bf16[1056,256]{1,0:T(8,128)(2,1)S(1)}, bf16[1056,256]{1,0:T(8,128)(2,1)S(1)}, u32[]{:S(2)}, u32[]{:S(2)}) collective-permute-start(bf16[1056,256]{1,0:T(8,128)(2,1)S(1)} %collective-permute-done.1.x2), channel_id=1, source_target_pairs={{0,16},{16,0},{1,17},{17,1},{2,18},{18,2},{3,19},{19,3},{4,20},{20... | collective-permute-start | bytes 1622024 | tf_op jit(solution)/shard_map/ppermute | solution.py:258
  28.1 0.0 collective-permute-done.2
  28.1 0.1 constant_dynamic-slice_fusion
  28.2 0.1 reduce_sum.28
  28.4 0.1 multiply_reduce_fusion
  28.5 0.1 subtract_select_fusion
  28.5 0.1 copy.14
  28.6 0.1 select_reduce_fusion
  28.7 0.1 pad_add_fusion.order
  28.8 0.9 collective-permute-done.3.x3
  29.7 0.0 copy-start.1
  29.7 0.8 copy-done.1
  30.5 22.2 %all-to-all-done.kv = bf16[16,2,64,128]{3,2,1,0:T(8,128)(2,1)S(1)} async-done(((bf16[16,2,64,128]{3,2,1,0:T(8,128)(2,1)}), bf16[16,2,64,128]{3,2,1,0:T(8,128)(2,1)S(1)}, u32[]{:S(2)}, u32[]{:S(2)}) %all-to-all-start) | async-done | bytes 524320 | tf_op jit(solution)/shard_map/all_to_all | solution.py:272
  52.8 0.0 copy-start.2
  52.8 1.0 copy-done.2
  53.8 8.9 %attention.1 = (bf16[16,2,64,128]{3,2,1,0:T(8,128)(2,1)}, bf16[2,512,256]{2,1,0:T(8,128)(2,1)S(1)}, bf16[2,512,256]{2,1,0:T(8,128)(2,1)S(1)}) custom-call(s32[32,16]{1,0:T(8,128)S(1)} %maximum_convert_fusion.mask, s32[8,17]{1,0:T(8,128)S(1)} %pad_add_fusion.order, bf16[16,2,64,128]{3,2,1,0:T(8,128)(2,1)S(1)} %all-to-all-done.kv, ...), custom_call_target="tpu_custom_call" | custom-call | flops 1789569664 | bytes 6291456 | tf_op jit(solution)/shard_map/attention/pallas_call | solution.py:216
  62.8 0.0 copy-start.3
  62.8 0.8 copy-done.3
  63.6 6.8 %all-to-all-start.1 = ((bf16[16,2,64,128]{3,2,1,0:T(8,128)(2,1)}), bf16[16,2,64,128]{3,2,1,0:T(8,128)(2,1)S(1)}, u32[]{:S(2)}, u32[]{:S(2)}) async-start(bf16[16,2,64,128]{3,2,1,0:T(8,128)(2,1)} %get-tuple-element.30), calls=%async_computation.1 | async-start | bytes 1048576 | tf_op jit(solution)/shard_map/all_to_all | solution.py:288
  70.4 0.0 copy-done.4
  70.4 3.0 %collective-permute-start.4 = (bf16[2,512,256]{2,1,0:T(8,128)(2,1)S(1)}, bf16[2,512,256]{2,1,0:T(8,128)(2,1)S(1)}, u32[]{:S(2)}, u32[]{:S(2)}) collective-permute-start(bf16[2,512,256]{2,1,0:T(8,128)(2,1)S(1)} %copy-done.4), channel_id=1, source_target_pairs={{0,16},{16,0},{1,17},{17,1},{2,18},{18,2},{3,19},{19,3},{4,20},{20... | collective-permute-start | bytes 1572872 | tf_op jit(solution)/shard_map/ppermute | solution.py:258
  73.4 1.5 %collective-permute-done.4 = bf16[2,512,256]{2,1,0:T(8,128)(2,1)S(1)} collective-permute-done((bf16[2,512,256]{2,1,0:T(8,128)(2,1)S(1)}, bf16[2,512,256]{2,1,0:T(8,128)(2,1)S(1)}, u32[]{:S(2)}, u32[]{:S(2)}) %collective-permute-start.4) | collective-permute-done | bytes 524320 | tf_op jit(solution)/shard_map/ppermute | solution.py:258
  74.9 0.1 halve.4
  75.0 2.2 %collective-permute-start.5 = (bf16[16,32,256]{2,1,0:T(8,128)(2,1)S(1)}, bf16[16,32,256]{2,1,0:T(8,128)(2,1)S(1)}, u32[]{:S(2)}, u32[]{:S(2)}) collective-permute-start(bf16[16,32,256]{2,1,0:T(8,128)(2,1)S(1)} %get-tuple-element.23), channel_id=1, source_target_pairs={{0,1},{1,0},{2,3},{3,2},{4,5},{5,4},{6,7},{7,6},{8,9},{9,8},{10,11... | collective-permute-start | bytes 786440 | tf_op jit(solution)/shard_map/ppermute | solution.py:143
  77.3 8.3 %collective-permute-done.5 = bf16[16,32,256]{2,1,0:T(8,128)(2,1)S(1)} collective-permute-done((bf16[16,32,256]{2,1,0:T(8,128)(2,1)S(1)}, bf16[16,32,256]{2,1,0:T(8,128)(2,1)S(1)}, u32[]{:S(2)}, u32[]{:S(2)}) %collective-permute-start.5) | collective-permute-done | bytes 262176 | tf_op jit(solution)/shard_map/ppermute | solution.py:143
  85.6 3.2 %collective-permute-start.6 = (bf16[8,32,256]{2,1,0:T(8,128)(2,1)S(1)}, bf16[8,32,256]{2,1,0:T(8,128)(2,1)S(1)}, u32[]{:S(2)}, u32[]{:S(2)}) collective-permute-start(bf16[8,32,256]{2,1,0:T(8,128)(2,1)S(1)} %get-tuple-element.25), channel_id=1, source_target_pairs={{0,2},{1,3},{2,0},{3,1},{4,6},{5,7},{6,4},{7,5},{8,10},{9,11},{10,... | collective-permute-start | bytes 393224 | tf_op jit(solution)/shard_map/ppermute | solution.py:143
  88.8 5.2 %collective-permute-done.6 = bf16[8,32,256]{2,1,0:T(8,128)(2,1)S(1)} collective-permute-done((bf16[8,32,256]{2,1,0:T(8,128)(2,1)S(1)}, bf16[8,32,256]{2,1,0:T(8,128)(2,1)S(1)}, u32[]{:S(2)}, u32[]{:S(2)}) %collective-permute-start.6) | collective-permute-done | bytes 131104 | tf_op jit(solution)/shard_map/ppermute | solution.py:143
  93.9 1.9 %collective-permute-start.7 = (bf16[4,32,256]{2,1,0:T(8,128)(2,1)S(1)}, bf16[4,32,256]{2,1,0:T(8,128)(2,1)S(1)}, u32[]{:S(2)}, u32[]{:S(2)}) collective-permute-start(bf16[4,32,256]{2,1,0:T(8,128)(2,1)S(1)} %get-tuple-element.27), channel_id=1, source_target_pairs={{0,4},{4,0},{8,12},{12,8},{1,5},{5,1},{9,13},{13,9},{2,6},{6,2},{1... | collective-permute-start | bytes 196616 | tf_op jit(solution)/shard_map/ppermute | solution.py:143
  95.9 4.2 %collective-permute-done.7 = bf16[4,32,256]{2,1,0:T(8,128)(2,1)S(1)} collective-permute-done((bf16[4,32,256]{2,1,0:T(8,128)(2,1)S(1)}, bf16[4,32,256]{2,1,0:T(8,128)(2,1)S(1)}, u32[]{:S(2)}, u32[]{:S(2)}) %collective-permute-start.7) | collective-permute-done | bytes 65568 | tf_op jit(solution)/shard_map/ppermute | solution.py:143
  100.1 3.8 %collective-permute-start.8 = (bf16[2,32,256]{2,1,0:T(8,128)(2,1)S(1)}, bf16[2,32,256]{2,1,0:T(8,128)(2,1)S(1)}, u32[]{:S(2)}, u32[]{:S(2)}) collective-permute-start(bf16[2,32,256]{2,1,0:T(8,128)(2,1)S(1)} %get-tuple-element.29), channel_id=1, source_target_pairs={{0,8},{4,12},{8,0},{12,4},{1,9},{5,13},{9,1},{13,5},{2,10},{6,14},... | collective-permute-start | bytes 98312 | tf_op jit(solution)/shard_map/ppermute | solution.py:143
  103.9 3.5 %collective-permute-done.8 = bf16[2,32,256]{2,1,0:T(8,128)(2,1)S(1)} collective-permute-done((bf16[2,32,256]{2,1,0:T(8,128)(2,1)S(1)}, bf16[2,32,256]{2,1,0:T(8,128)(2,1)S(1)}, u32[]{:S(2)}, u32[]{:S(2)}) %collective-permute-start.8) | collective-permute-done | bytes 32800 | tf_op jit(solution)/shard_map/ppermute | solution.py:143
  107.5 3.5 %collective-permute-start.9 = (bf16[32,256]{1,0:T(8,128)(2,1)S(1)}, bf16[32,256]{1,0:T(8,128)(2,1)S(1)}, u32[]{:S(2)}, u32[]{:S(2)}) collective-permute-start(bf16[32,256]{1,0:T(8,128)(2,1)S(1)} %fusion.2), channel_id=1, source_target_pairs={{0,32},{32,0},{64,96},{96,64},{128,160},{160,128},{192,224},{224,1... | collective-permute-start | bytes 49160 | tf_op jit(solution)/shard_map/ppermute | solution.py:262
  111.0 2.1 %collective-permute-done.9 = bf16[32,256]{1,0:T(8,128)(2,1)S(1)} collective-permute-done((bf16[32,256]{1,0:T(8,128)(2,1)S(1)}, bf16[32,256]{1,0:T(8,128)(2,1)S(1)}, u32[]{:S(2)}, u32[]{:S(2)}) %collective-permute-start.9) | collective-permute-done | bytes 16416 | tf_op jit(solution)/shard_map/ppermute | solution.py:262
  113.1 0.6 fusion.1
  113.7 0.0 all-to-all-done.1.back
  113.7 0.9 place.1
  (14 shorter events, 0.2 us)
Async XLA Ops:
  3.3 20.2 %copy-start = (bf16[1056,256]{1,0:T(8,128)(2,1)S(1)}, bf16[1056,256]{1,0:T(8,128)(2,1)}, u32[]{:S(2)}) copy-start(bf16[1056,256]{1,0:T(8,128)(2,1)} %get-tuple-element.18.x0) | copy-start | bytes 1622020
  3.3 20.3 %collective-permute-start.1 = (bf16[1056,256]{1,0:T(8,128)(2,1)}, bf16[1056,256]{1,0:T(8,128)(2,1)S(1)}, u32[]{:S(2)}, u32[]{:S(2)}) collective-permute-start(bf16[1056,256]{1,0:T(8,128)(2,1)} %get-tuple-element.18.x0), channel_id=1, source_target_pairs={{0,32},{32,0},{64,96},{96,64},{128,160},{160,128},{192,224},{224,1... | collective-permute-start | bytes 1622024 | tf_op jit(solution)/shard_map/ppermute | solution.py:262
  7.2 18.5 %collective-permute-start = (bf16[1056,256]{1,0:T(8,128)(2,1)}, bf16[1056,256]{1,0:T(8,128)(2,1)S(1)}, u32[]{:S(2)}, u32[]{:S(2)}) collective-permute-start(bf16[1056,256]{1,0:T(8,128)(2,1)} %get-tuple-element.18.x0), channel_id=1, source_target_pairs={{0,16},{16,0},{1,17},{17,1},{2,18},{18,2},{3,19},{19,3},{4,20},{20... | collective-permute-start | bytes 1622024 | tf_op jit(solution)/shard_map/ppermute | solution.py:258
  9.2 43.6 %all-to-all-start = ((bf16[16,2,64,128]{3,2,1,0:T(8,128)(2,1)}), bf16[16,2,64,128]{3,2,1,0:T(8,128)(2,1)S(1)}, u32[]{:S(2)}, u32[]{:S(2)}) async-start(bf16[16,2,64,128]{3,2,1,0:T(8,128)(2,1)} %get-tuple-element.19), calls=%async_computation | async-start | bytes 1048576 | tf_op jit(solution)/shard_map/all_to_all | solution.py:272
  23.6 4.5 %collective-permute-start.2 = (bf16[8,256]{1,0:T(8,128)(2,1)S(1)}, bf16[8,256]{1,0:T(8,128)(2,1)S(1)}, u32[]{:S(2)}, u32[]{:S(2)}) collective-permute-start(bf16[8,256]{1,0:T(8,128)(2,1)S(1)} %slice.22), channel_id=1, source_target_pairs={{0,16},{16,0},{1,17},{17,1},{2,18},{18,2},{3,19},{19,3},{4,20},{20... | collective-permute-start | bytes 12296 | tf_op jit(solution)/shard_map/ppermute | solution.py:258
  25.9 3.8 %collective-permute-start.3 = (bf16[1056,256]{1,0:T(8,128)(2,1)S(1)}, bf16[1056,256]{1,0:T(8,128)(2,1)S(1)}, u32[]{:S(2)}, u32[]{:S(2)}) collective-permute-start(bf16[1056,256]{1,0:T(8,128)(2,1)S(1)} %collective-permute-done.1.x2), channel_id=1, source_target_pairs={{0,16},{16,0},{1,17},{17,1},{2,18},{18,2},{3,19},{19,3},{4,20},{20... | collective-permute-start | bytes 1622024 | tf_op jit(solution)/shard_map/ppermute | solution.py:258
  29.7 0.8 copy-start.1
  52.8 1.0 copy-start.2
  62.8 0.8 copy-start.3
  63.6 6.8 %copy-start.4 = (bf16[2,512,256]{2,1,0:T(8,128)(2,1)S(1)}, bf16[2,512,256]{2,1,0:T(8,128)(2,1)}, u32[]{:S(2)}) copy-start(bf16[2,512,256]{2,1,0:T(8,128)(2,1)} %copy-done.3) | copy-start | bytes 1572868
  63.6 50.1 %all-to-all-start.1 = ((bf16[16,2,64,128]{3,2,1,0:T(8,128)(2,1)}), bf16[16,2,64,128]{3,2,1,0:T(8,128)(2,1)S(1)}, u32[]{:S(2)}, u32[]{:S(2)}) async-start(bf16[16,2,64,128]{3,2,1,0:T(8,128)(2,1)} %get-tuple-element.30), calls=%async_computation.1 | async-start | bytes 1048576 | tf_op jit(solution)/shard_map/all_to_all | solution.py:288
  70.4 4.5 %collective-permute-start.4 = (bf16[2,512,256]{2,1,0:T(8,128)(2,1)S(1)}, bf16[2,512,256]{2,1,0:T(8,128)(2,1)S(1)}, u32[]{:S(2)}, u32[]{:S(2)}) collective-permute-start(bf16[2,512,256]{2,1,0:T(8,128)(2,1)S(1)} %copy-done.4), channel_id=1, source_target_pairs={{0,16},{16,0},{1,17},{17,1},{2,18},{18,2},{3,19},{19,3},{4,20},{20... | collective-permute-start | bytes 1572872 | tf_op jit(solution)/shard_map/ppermute | solution.py:258
  75.0 10.5 %collective-permute-start.5 = (bf16[16,32,256]{2,1,0:T(8,128)(2,1)S(1)}, bf16[16,32,256]{2,1,0:T(8,128)(2,1)S(1)}, u32[]{:S(2)}, u32[]{:S(2)}) collective-permute-start(bf16[16,32,256]{2,1,0:T(8,128)(2,1)S(1)} %get-tuple-element.23), channel_id=1, source_target_pairs={{0,1},{1,0},{2,3},{3,2},{4,5},{5,4},{6,7},{7,6},{8,9},{9,8},{10,11... | collective-permute-start | bytes 786440 | tf_op jit(solution)/shard_map/ppermute | solution.py:143
  85.6 8.4 %collective-permute-start.6 = (bf16[8,32,256]{2,1,0:T(8,128)(2,1)S(1)}, bf16[8,32,256]{2,1,0:T(8,128)(2,1)S(1)}, u32[]{:S(2)}, u32[]{:S(2)}) collective-permute-start(bf16[8,32,256]{2,1,0:T(8,128)(2,1)S(1)} %get-tuple-element.25), channel_id=1, source_target_pairs={{0,2},{1,3},{2,0},{3,1},{4,6},{5,7},{6,4},{7,5},{8,10},{9,11},{10,... | collective-permute-start | bytes 393224 | tf_op jit(solution)/shard_map/ppermute | solution.py:143
  93.9 6.2 %collective-permute-start.7 = (bf16[4,32,256]{2,1,0:T(8,128)(2,1)S(1)}, bf16[4,32,256]{2,1,0:T(8,128)(2,1)S(1)}, u32[]{:S(2)}, u32[]{:S(2)}) collective-permute-start(bf16[4,32,256]{2,1,0:T(8,128)(2,1)S(1)} %get-tuple-element.27), channel_id=1, source_target_pairs={{0,4},{4,0},{8,12},{12,8},{1,5},{5,1},{9,13},{13,9},{2,6},{6,2},{1... | collective-permute-start | bytes 196616 | tf_op jit(solution)/shard_map/ppermute | solution.py:143
  100.1 7.3 %collective-permute-start.8 = (bf16[2,32,256]{2,1,0:T(8,128)(2,1)S(1)}, bf16[2,32,256]{2,1,0:T(8,128)(2,1)S(1)}, u32[]{:S(2)}, u32[]{:S(2)}) collective-permute-start(bf16[2,32,256]{2,1,0:T(8,128)(2,1)S(1)} %get-tuple-element.29), channel_id=1, source_target_pairs={{0,8},{4,12},{8,0},{12,4},{1,9},{5,13},{9,1},{13,5},{2,10},{6,14},... | collective-permute-start | bytes 98312 | tf_op jit(solution)/shard_map/ppermute | solution.py:143
  107.5 5.6 %collective-permute-start.9 = (bf16[32,256]{1,0:T(8,128)(2,1)S(1)}, bf16[32,256]{1,0:T(8,128)(2,1)S(1)}, u32[]{:S(2)}, u32[]{:S(2)}) collective-permute-start(bf16[32,256]{1,0:T(8,128)(2,1)S(1)} %fusion.2), channel_id=1, source_target_pairs={{0,32},{32,0},{64,96},{96,64},{128,160},{160,128},{192,224},{224,1... | collective-permute-start | bytes 49160 | tf_op jit(solution)/shard_map/ppermute | solution.py:262

commit v3 on v2

--- a/solution.py
+++ b/solution.py
@@ -143,28 +143,56 @@
     return lax.ppermute(value, axis, [(i, i ^ distance) for i in range(4)])
 
 
-def attention_kernel(mask, order, kv, x0, x1, x2, x3, dkv, keep, send,
-                     xs, norm, dots, kbuf, vbuf, dk, dv, dq, sems):
+def stage_kernel(x0, x1, x2, x3, qs, gs, qt, gt, norm, dots):
+    for s, x in enumerate((x0, x1, x2, x3)):
+        aux = x[2 * SLAB_QUERIES:].astype(f32)
+        aux = aux[:8] + aux[8:16]
+        for l in range(2):
+            h, lanes = 2 * s + l, slice(l * HEAD_SIZE, (l + 1) * HEAD_SIZE)
+            q, g = x[:SLAB_QUERIES, lanes], x[SLAB_QUERIES:2 * SLAB_QUERIES, lanes]
+            qs[h], gs[h], qt[h], gt[h] = q, g, q.T, g.T
+            dots[h] = jnp.concatenate([aux[2 * l:2 * l + 1], aux[2 * l + 1:2 * l + 2]], axis=1)
+            norm[h] = jnp.concatenate([aux[2 * l + 4:2 * l + 5], aux[2 * l + 5:2 * l + 6]], axis=1)
+
+
+def staged(xs):
+    vmem = pl.BlockSpec(memory_space=pltpu.VMEM)
+    heads = 2 * SLOTS
+    return pl.pallas_call(
+        stage_kernel,
+        out_shape=(
+            (jax.ShapeDtypeStruct((heads, SLAB_QUERIES, HEAD_SIZE), bf16),) * 2
+            + (jax.ShapeDtypeStruct((heads, HEAD_SIZE, SLAB_QUERIES), bf16),) * 2
+            + (jax.ShapeDtypeStruct((heads, 1, SLAB_QUERIES), f32),) * 2
+        ),
+        in_specs=[vmem] * SLOTS,
+        out_specs=(vmem,) * 6,
+        compiler_params=pltpu.CompilerParams(vmem_limit_bytes=16 * 2**20),
+        name="stage",
+    )(*xs)
+
+
+def attention_kernel(mask, order, kv, q_in, g_in, qt_in, gt_in, norm, dots, dkv, keep, send,
+                     qs, gs, qt, gt, kbuf, vbuf, dk, dv, dq, sems):
     scale = HEAD_SIZE ** -0.5
-    copies = [pltpu.make_async_copy(x, xs.at[s], sems.at[s]) for s, x in enumerate((x0, x1, x2, x3))]
-    for copy in copies:
-        copy.start()
+
+    def fetches(h):
+        pairs = ((qt_in, qt), (gt_in, gt), (g_in, gs), (q_in, qs))
+        return [
+            pltpu.make_async_copy(source.at[h], target.at[h], sems.at[h, i])
+            for i, (source, target) in enumerate(pairs)
+        ]
+
+    for h in range(2 * SLOTS):
+        for copy in fetches(h):
+            copy.start()
     dk[...] = jnp.zeros_like(dk)
     dv[...] = jnp.zeros_like(dv)
     dq[...] = jnp.zeros_like(dq)
 
     def head(h, _):
-        for s, copy in enumerate(copies):
-            @pl.when(h == 2 * s)
-            def _():
-                copy.wait()
-                aux = xs[s, 2 * SLAB_QUERIES:, :].astype(f32)
-                aux = aux[:8] + aux[8:16]
-                for l in range(2):
-                    dots[2 * s + l] = jnp.concatenate([aux[2 * l:2 * l + 1], aux[2 * l + 1:2 * l + 2]], axis=1)
-                    norm[2 * s + l] = jnp.concatenate([aux[2 * l + 4:2 * l + 5], aux[2 * l + 5:2 * l + 6]], axis=1)
-
-        s, lanes = h // 2, pl.ds(pl.multiple_of((h % 2) * HEAD_SIZE, HEAD_SIZE), HEAD_SIZE)
+        for copy in fetches(h):
+            copy.wait()
 
         def turn(t, _):
             picked = [order[h, t * PICK + j] for j in range(PICK)]
@@ -181,10 +209,10 @@
                 )
                 rows.append(jnp.broadcast_to(row, (HALF, SLAB_QUERIES)))
             bias = jnp.concatenate(rows, axis=0)
-            q, g = xs[s, :SLAB_QUERIES, lanes], xs[s, SLAB_QUERIES:2 * SLAB_QUERIES, lanes]
-            scores = dot(kbuf[...], q, ((1,), (1,)))
+            q, g = qs[h], gs[h]
+            scores = dot(kbuf[...], qt[h], ((1,), (0,)))
             w = jnp.exp2(scores * (scale * LOG2E) + bias)
-            gw = dot(vbuf[...], g, ((1,), (1,)))
+            gw = dot(vbuf[...], gt[h], ((1,), (0,)))
             ds = (w * (gw - dots[h])).astype(bf16)
             dv_part = dot(w.astype(bf16), g, ((1,), (0,)))
             dk_part = dot(ds, q, ((1,), (0,)))
@@ -220,20 +248,21 @@
             jax.ShapeDtypeStruct((2, *rows), bf16),
             jax.ShapeDtypeStruct((2, *rows), bf16),
         ),
-        in_specs=[pl.BlockSpec(memory_space=pltpu.SMEM)] * 2 + [vmem] + [pl.BlockSpec(memory_space=pl.ANY)] * 4,
+        in_specs=[pl.BlockSpec(memory_space=pltpu.SMEM)] * 2 + [vmem] + [pl.BlockSpec(memory_space=pl.ANY)] * 4 + [vmem] * 2,
         out_specs=(vmem, vmem, vmem),
         scratch_shapes=[
-            pltpu.VMEM((SLOTS, PACKED, 2 * HEAD_SIZE), bf16),
-            pltpu.VMEM((2 * SLOTS, 1, SLAB_QUERIES), f32),
-            pltpu.VMEM((2 * SLOTS, 1, SLAB_QUERIES), f32),
+            pltpu.VMEM((2 * SLOTS, SLAB_QUERIES, HEAD_SIZE), bf16),
+            pltpu.VMEM((2 * SLOTS, SLAB_QUERIES, HEAD_SIZE), bf16),
+            pltpu.VMEM((2 * SLOTS, HEAD_SIZE, SLAB_QUERIES), bf16),
+            pltpu.VMEM((2 * SLOTS, HEAD_SIZE, SLAB_QUERIES), bf16),
             pltpu.VMEM((PICK * HALF, HEAD_SIZE), bf16),
             pltpu.VMEM((PICK * HALF, HEAD_SIZE), bf16),
             pltpu.VMEM((Z, HALF, HEAD_SIZE), f32),
             pltpu.VMEM((Z, HALF, HEAD_SIZE), f32),
             pltpu.VMEM((2 * SLOTS, HEAD_SIZE, SLAB_QUERIES), f32),
-            pltpu.SemaphoreType.DMA((SLOTS,)),
+            pltpu.SemaphoreType.DMA((2 * SLOTS, 4)),
         ],
-        compiler_params=pltpu.CompilerParams(vmem_limit_bytes=28 * 2**20),
+        compiler_params=pltpu.CompilerParams(vmem_limit_bytes=51 * 2**20),
         cost_estimate=pl.CostEstimate(
             flops=5 * 2 * 4096 * 1024 * 128 // 3,
             bytes_accessed=6 * 2**20,
@@ -274,13 +303,14 @@
     x3 = other_core(x2)
     slots = (x0, x1, x2, x3)
     at = 2 * SLAB_QUERIES + 16
+    operands = staged(slots)
     attended = [a[at:at + 8] for a in slots[:3]]
     attended.append(other_core(attended[2]))
     mask = jnp.concatenate(
         [lax.dynamic_slice_in_dim(a, core * Z, Z, 1) for a in attended]
     ).astype(jnp.int32)
 
-    dkv, keep, send = attention(mask, attended_first(mask), kv, slots)
+    dkv, keep, send = attention(mask, attended_first(mask), kv, operands)
 
     got = other_core(send)
     own, sent = halve(x % 2, keep, got)

time: 115 us -> 114 us (level)
  waiting for transfers between devices: 47.9 us -> 44 us
  local copies, waits for them, and re-layouts: 3.05 us -> 4.35 us
    all_to_all x1, waiting for transfers between devices: 22.2 us -> 18.4 us  [compute(): kv = lax.all_to_all(own_kv, 'z', 0, 0, tiled=True)]
    unnamed x10, local copies, waits for them, and re-layouts: 2.64 us -> 3.94 us
  transfers between devices with their start and end apart: 12 -> 12, of which waited for: 8 -> 8; matrix products, arithmetic and copies ran while one was open for 1% -> 1% of each run, Pallas kernels for 0% -> 1%
where the time goes in v3:
time: 114 us; the launch traced here: 113 us
  starting transfers between devices  48.9 us (43%)
  waiting for transfers between devices  44 us (39%)
  Pallas kernels  13.8 us (12%)
  local copies, waits for them, and re-layouts  4.35 us (4%)
    ppermute x4, waiting for transfers between devices, across(): return lax.ppermute(value, axis, [(i, i ^ distance) for i in range(4)])  21 us
    all_to_all x1, waiting for transfers between devices, compute(): kv = lax.all_to_all(own_kv, 'z', 0, 0, tiled=True)  18.4 us
    all_to_all x1, starting transfers between devices, compute(): kv = lax.all_to_all(own_kv, 'z', 0, 0, tiled=True)  14.3 us
    ppermute x4, starting transfers between devices, across(): return lax.ppermute(value, axis, [(i, i ^ distance) for i in range(4)])  11.2 us
    pallas_call x1, Pallas kernels, attention(): pl.pallas_call(attention_kernel, out_shape=(jax.ShapeDtypeStruct((Z, 2, H...  9.41 us
    ppermute x4, starting transfers between devices, other_core(): return lax.ppermute(value, 'core', [(0, 1), (1, 0)])  9.21 us
    ppermute x2, starting transfers between devices, other_chip(): return lax.ppermute(value, 'z', [(z, z ^ 1) for z in range(Z)])  7.5 us
    all_to_all x1, starting transfers between devices, compute(): back = lax.all_to_all(dkv, 'z', 0, 0, tiled=True)  6.67 us
  transfers between devices with their start and end apart: 12, of which 8 were waited for; matrix products, arithmetic and copies ran while one was open for 1% of the time, Pallas kernels for 1%

profile of v3, /device:TPU:10, one launch (start us, length us, event | category | flops | bytes accessed | tf_op | source)
XLA Modules:
  0.0 113.1 jit_solution(9866723451434104313)
XLA Ops:
  0.6 2.6 %prepare.1 = (bf16[16,2,64,128]{3,2,1,0:T(8,128)(2,1)}, bf16[1056,256]{1,0:T(8,128)(2,1)}) custom-call(s32[1]{0:T(128)} %bitcast.4.rep, bf16[512,256]{1,0:T(8,128)(2,1)} %queries.1, bf16[128,1024]{1,0:T(8,128)(2,1)} %keys.1, bf16[128,1024]{1,0:T(8,128)(2,1)} %values.1, bf16[512,256]{1,0:T(8,128)(2,1)} %output.1, bf16[512,256]{1,0:T(8,128)(2,1)} %cotangent.1, ...), custom_call_target="tpu_custom_call" | custom-call | tf_op jit(solution)/shard_map/prepare/pallas_call | solution.py:82
  3.3 0.0 copy-start
  3.3 4.0 %collective-permute-start.1 = (bf16[1056,256]{1,0:T(8,128)(2,1)}, bf16[1056,256]{1,0:T(8,128)(2,1)S(1)}, u32[]{:S(2)}, u32[]{:S(2)}) collective-permute-start(bf16[1056,256]{1,0:T(8,128)(2,1)} %get-tuple-element.24.x0), channel_id=1, source_target_pairs={{0,32},{32,0},{64,96},{96,64},{128,160},{160,128},{192,224},{224,1... | collective-permute-start | bytes 1622024 | tf_op jit(solution)/shard_map/ppermute | solution.py:291
  7.2 1.9 %collective-permute-start = (bf16[1056,256]{1,0:T(8,128)(2,1)}, bf16[1056,256]{1,0:T(8,128)(2,1)S(1)}, u32[]{:S(2)}, u32[]{:S(2)}) collective-permute-start(bf16[1056,256]{1,0:T(8,128)(2,1)} %get-tuple-element.24.x0), channel_id=1, source_target_pairs={{0,16},{16,0},{1,17},{17,1},{2,18},{18,2},{3,19},{19,3},{4,20},{20... | collective-permute-start | bytes 1622024 | tf_op jit(solution)/shard_map/ppermute | solution.py:287
  9.2 14.3 %all-to-all-start = ((bf16[16,2,64,128]{3,2,1,0:T(8,128)(2,1)}), bf16[16,2,64,128]{3,2,1,0:T(8,128)(2,1)S(1)}, u32[]{:S(2)}, u32[]{:S(2)}) async-start(bf16[16,2,64,128]{3,2,1,0:T(8,128)(2,1)} %get-tuple-element.25), calls=%async_computation | async-start | bytes 1048576 | tf_op jit(solution)/shard_map/all_to_all | solution.py:301
  23.5 0.0 copy-done
  23.5 0.1 constant_dynamic-slice_fusion.3
  23.6 0.0 collective-permute-done.1.x2
  23.6 2.1 %collective-permute-start.2 = (bf16[8,256]{1,0:T(8,128)(2,1)S(1)}, bf16[8,256]{1,0:T(8,128)(2,1)S(1)}, u32[]{:S(2)}, u32[]{:S(2)}) collective-permute-start(bf16[8,256]{1,0:T(8,128)(2,1)S(1)} %slice.22), channel_id=1, source_target_pairs={{0,16},{16,0},{1,17},{17,1},{2,18},{18,2},{3,19},{19,3},{4,20},{20... | collective-permute-start | bytes 12296 | tf_op jit(solution)/shard_map/ppermute | solution.py:287
  25.7 0.0 collective-permute-done.x1
  25.7 0.1 constant_dynamic-slice_fusion.1
  25.8 0.1 constant_dynamic-slice_fusion.2
  25.9 2.2 %collective-permute-start.3 = (bf16[1056,256]{1,0:T(8,128)(2,1)S(1)}, bf16[1056,256]{1,0:T(8,128)(2,1)S(1)}, u32[]{:S(2)}, u32[]{:S(2)}) collective-permute-start(bf16[1056,256]{1,0:T(8,128)(2,1)S(1)} %collective-permute-done.1.x2), channel_id=1, source_target_pairs={{0,16},{16,0},{1,17},{17,1},{2,18},{18,2},{3,19},{19,3},{4,20},{20... | collective-permute-start | bytes 1622024 | tf_op jit(solution)/shard_map/ppermute | solution.py:287
  28.1 0.0 collective-permute-done.2
  28.1 0.1 constant_dynamic-slice_fusion
  28.2 0.1 reduce_sum.28
  28.3 0.1 multiply_reduce_fusion
  28.4 0.1 subtract_select_fusion
  28.5 0.1 copy.14
  28.6 0.1 select_reduce_fusion
  28.7 0.1 pad_add_fusion.order
  28.8 0.9 collective-permute-done.3.x3
  29.7 0.7 stage.1
  30.4 0.0 copy-start.1
  30.4 1.0 copy-done.1
  31.4 0.0 copy-start.2
  31.4 1.0 copy-done.2
  32.4 1.0 copy-done.3
  33.3 1.0 copy-done.4
  34.3 18.4 %all-to-all-done.kv = bf16[16,2,64,128]{3,2,1,0:T(8,128)(2,1)S(1)} async-done(((bf16[16,2,64,128]{3,2,1,0:T(8,128)(2,1)}), bf16[16,2,64,128]{3,2,1,0:T(8,128)(2,1)S(1)}, u32[]{:S(2)}, u32[]{:S(2)}) %all-to-all-start) | async-done | bytes 524320 | tf_op jit(solution)/shard_map/all_to_all | solution.py:301
  52.8 9.4 %attention.1 = (bf16[16,2,64,128]{3,2,1,0:T(8,128)(2,1)}, bf16[2,512,256]{2,1,0:T(8,128)(2,1)S(1)}, bf16[2,512,256]{2,1,0:T(8,128)(2,1)S(1)}) custom-call(s32[32,16]{1,0:T(8,128)S(1)} %maximum_convert_fusion.mask, s32[8,17]{1,0:T(8,128)S(1)} %pad_add_fusion.order, bf16[16,2,64,128]{3,2,1,0:T(8,128)(2,1)S(1)} %all-to-all-done.kv, ...), custom_call_target="tpu_custom_call" | custom-call | flops 1789569664 | bytes 6291456 | tf_op jit(solution)/shard_map/attention/pallas_call | solution.py:244
  62.2 6.7 %all-to-all-start.1 = ((bf16[16,2,64,128]{3,2,1,0:T(8,128)(2,1)}), bf16[16,2,64,128]{3,2,1,0:T(8,128)(2,1)S(1)}, u32[]{:S(2)}, u32[]{:S(2)}) async-start(bf16[16,2,64,128]{3,2,1,0:T(8,128)(2,1)} %get-tuple-element.42), calls=%async_computation.1 | async-start | bytes 1048576 | tf_op jit(solution)/shard_map/all_to_all | solution.py:318
  68.8 3.0 %collective-permute-start.4 = (bf16[2,512,256]{2,1,0:T(8,128)(2,1)S(1)}, bf16[2,512,256]{2,1,0:T(8,128)(2,1)S(1)}, u32[]{:S(2)}, u32[]{:S(2)}) collective-permute-start(bf16[2,512,256]{2,1,0:T(8,128)(2,1)S(1)} %get-tuple-element.33), channel_id=1, source_target_pairs={{0,16},{16,0},{1,17},{17,1},{2,18},{18,2},{3,19},{19,3},{4,20},{20... | collective-permute-start | bytes 1572872 | tf_op jit(solution)/shard_map/ppermute | solution.py:287
  71.8 1.5 %collective-permute-done.4 = bf16[2,512,256]{2,1,0:T(8,128)(2,1)S(1)} collective-permute-done((bf16[2,512,256]{2,1,0:T(8,128)(2,1)S(1)}, bf16[2,512,256]{2,1,0:T(8,128)(2,1)S(1)}, u32[]{:S(2)}, u32[]{:S(2)}) %collective-permute-start.4) | collective-permute-done | bytes 524320 | tf_op jit(solution)/shard_map/ppermute | solution.py:287
  73.3 0.1 halve.4
  73.5 2.2 %collective-permute-start.5 = (bf16[16,32,256]{2,1,0:T(8,128)(2,1)S(1)}, bf16[16,32,256]{2,1,0:T(8,128)(2,1)S(1)}, u32[]{:S(2)}, u32[]{:S(2)}) collective-permute-start(bf16[16,32,256]{2,1,0:T(8,128)(2,1)S(1)} %get-tuple-element.35), channel_id=1, source_target_pairs={{0,1},{1,0},{2,3},{3,2},{4,5},{5,4},{6,7},{7,6},{8,9},{9,8},{10,11... | collective-permute-start | bytes 786440 | tf_op jit(solution)/shard_map/ppermute | solution.py:143
  75.7 8.3 %collective-permute-done.5 = bf16[16,32,256]{2,1,0:T(8,128)(2,1)S(1)} collective-permute-done((bf16[16,32,256]{2,1,0:T(8,128)(2,1)S(1)}, bf16[16,32,256]{2,1,0:T(8,128)(2,1)S(1)}, u32[]{:S(2)}, u32[]{:S(2)}) %collective-permute-start.5) | collective-permute-done | bytes 262176 | tf_op jit(solution)/shard_map/ppermute | solution.py:143
  84.0 3.2 %collective-permute-start.6 = (bf16[8,32,256]{2,1,0:T(8,128)(2,1)S(1)}, bf16[8,32,256]{2,1,0:T(8,128)(2,1)S(1)}, u32[]{:S(2)}, u32[]{:S(2)}) collective-permute-start(bf16[8,32,256]{2,1,0:T(8,128)(2,1)S(1)} %get-tuple-element.37), channel_id=1, source_target_pairs={{0,2},{1,3},{2,0},{3,1},{4,6},{5,7},{6,4},{7,5},{8,10},{9,11},{10,... | collective-permute-start | bytes 393224 | tf_op jit(solution)/shard_map/ppermute | solution.py:143
  87.2 5.1 %collective-permute-done.6 = bf16[8,32,256]{2,1,0:T(8,128)(2,1)S(1)} collective-permute-done((bf16[8,32,256]{2,1,0:T(8,128)(2,1)S(1)}, bf16[8,32,256]{2,1,0:T(8,128)(2,1)S(1)}, u32[]{:S(2)}, u32[]{:S(2)}) %collective-permute-start.6) | collective-permute-done | bytes 131104 | tf_op jit(solution)/shard_map/ppermute | solution.py:143
  92.4 1.9 %collective-permute-start.7 = (bf16[4,32,256]{2,1,0:T(8,128)(2,1)S(1)}, bf16[4,32,256]{2,1,0:T(8,128)(2,1)S(1)}, u32[]{:S(2)}, u32[]{:S(2)}) collective-permute-start(bf16[4,32,256]{2,1,0:T(8,128)(2,1)S(1)} %get-tuple-element.39), channel_id=1, source_target_pairs={{0,4},{4,0},{8,12},{12,8},{1,5},{5,1},{9,13},{13,9},{2,6},{6,2},{1... | collective-permute-start | bytes 196616 | tf_op jit(solution)/shard_map/ppermute | solution.py:143
  94.3 4.2 %collective-permute-done.7 = bf16[4,32,256]{2,1,0:T(8,128)(2,1)S(1)} collective-permute-done((bf16[4,32,256]{2,1,0:T(8,128)(2,1)S(1)}, bf16[4,32,256]{2,1,0:T(8,128)(2,1)S(1)}, u32[]{:S(2)}, u32[]{:S(2)}) %collective-permute-start.7) | collective-permute-done | bytes 65568 | tf_op jit(solution)/shard_map/ppermute | solution.py:143
  98.5 3.8 %collective-permute-start.8 = (bf16[2,32,256]{2,1,0:T(8,128)(2,1)S(1)}, bf16[2,32,256]{2,1,0:T(8,128)(2,1)S(1)}, u32[]{:S(2)}, u32[]{:S(2)}) collective-permute-start(bf16[2,32,256]{2,1,0:T(8,128)(2,1)S(1)} %get-tuple-element.41), channel_id=1, source_target_pairs={{0,8},{4,12},{8,0},{12,4},{1,9},{5,13},{9,1},{13,5},{2,10},{6,14},... | collective-permute-start | bytes 98312 | tf_op jit(solution)/shard_map/ppermute | solution.py:143
  102.4 3.5 %collective-permute-done.8 = bf16[2,32,256]{2,1,0:T(8,128)(2,1)S(1)} collective-permute-done((bf16[2,32,256]{2,1,0:T(8,128)(2,1)S(1)}, bf16[2,32,256]{2,1,0:T(8,128)(2,1)S(1)}, u32[]{:S(2)}, u32[]{:S(2)}) %collective-permute-start.8) | collective-permute-done | bytes 32800 | tf_op jit(solution)/shard_map/ppermute | solution.py:143
  105.9 3.5 %collective-permute-start.9 = (bf16[32,256]{1,0:T(8,128)(2,1)S(1)}, bf16[32,256]{1,0:T(8,128)(2,1)S(1)}, u32[]{:S(2)}, u32[]{:S(2)}) collective-permute-start(bf16[32,256]{1,0:T(8,128)(2,1)S(1)} %fusion.2), channel_id=1, source_target_pairs={{0,32},{32,0},{64,96},{96,64},{128,160},{160,128},{192,224},{224,1... | collective-permute-start | bytes 49160 | tf_op jit(solution)/shard_map/ppermute | solution.py:291
  109.4 2.1 %collective-permute-done.9 = bf16[32,256]{1,0:T(8,128)(2,1)S(1)} collective-permute-done((bf16[32,256]{1,0:T(8,128)(2,1)S(1)}, bf16[32,256]{1,0:T(8,128)(2,1)S(1)}, u32[]{:S(2)}, u32[]{:S(2)}) %collective-permute-start.9) | collective-permute-done | bytes 16416 | tf_op jit(solution)/shard_map/ppermute | solution.py:291
  111.5 0.6 fusion.1
  112.1 0.0 all-to-all-done.1.back
  112.1 0.9 place.1
  (15 shorter events, 0.2 us)
Async XLA Ops:
  3.3 20.2 %copy-start = (bf16[1056,256]{1,0:T(8,128)(2,1)S(1)}, bf16[1056,256]{1,0:T(8,128)(2,1)}, u32[]{:S(2)}) copy-start(bf16[1056,256]{1,0:T(8,128)(2,1)} %get-tuple-element.24.x0) | copy-start | bytes 1622020
  3.3 20.3 %collective-permute-start.1 = (bf16[1056,256]{1,0:T(8,128)(2,1)}, bf16[1056,256]{1,0:T(8,128)(2,1)S(1)}, u32[]{:S(2)}, u32[]{:S(2)}) collective-permute-start(bf16[1056,256]{1,0:T(8,128)(2,1)} %get-tuple-element.24.x0), channel_id=1, source_target_pairs={{0,32},{32,0},{64,96},{96,64},{128,160},{160,128},{192,224},{224,1... | collective-permute-start | bytes 1622024 | tf_op jit(solution)/shard_map/ppermute | solution.py:291
  7.2 18.5 %collective-permute-start = (bf16[1056,256]{1,0:T(8,128)(2,1)}, bf16[1056,256]{1,0:T(8,128)(2,1)S(1)}, u32[]{:S(2)}, u32[]{:S(2)}) collective-permute-start(bf16[1056,256]{1,0:T(8,128)(2,1)} %get-tuple-element.24.x0), channel_id=1, source_target_pairs={{0,16},{16,0},{1,17},{17,1},{2,18},{18,2},{3,19},{19,3},{4,20},{20... | collective-permute-start | bytes 1622024 | tf_op jit(solution)/shard_map/ppermute | solution.py:287
  9.2 43.6 %all-to-all-start = ((bf16[16,2,64,128]{3,2,1,0:T(8,128)(2,1)}), bf16[16,2,64,128]{3,2,1,0:T(8,128)(2,1)S(1)}, u32[]{:S(2)}, u32[]{:S(2)}) async-start(bf16[16,2,64,128]{3,2,1,0:T(8,128)(2,1)} %get-tuple-element.25), calls=%async_computation | async-start | bytes 1048576 | tf_op jit(solution)/shard_map/all_to_all | solution.py:301
  23.6 4.5 %collective-permute-start.2 = (bf16[8,256]{1,0:T(8,128)(2,1)S(1)}, bf16[8,256]{1,0:T(8,128)(2,1)S(1)}, u32[]{:S(2)}, u32[]{:S(2)}) collective-permute-start(bf16[8,256]{1,0:T(8,128)(2,1)S(1)} %slice.22), channel_id=1, source_target_pairs={{0,16},{16,0},{1,17},{17,1},{2,18},{18,2},{3,19},{19,3},{4,20},{20... | collective-permute-start | bytes 12296 | tf_op jit(solution)/shard_map/ppermute | solution.py:287
  25.9 3.8 %collective-permute-start.3 = (bf16[1056,256]{1,0:T(8,128)(2,1)S(1)}, bf16[1056,256]{1,0:T(8,128)(2,1)S(1)}, u32[]{:S(2)}, u32[]{:S(2)}) collective-permute-start(bf16[1056,256]{1,0:T(8,128)(2,1)S(1)} %collective-permute-done.1.x2), channel_id=1, source_target_pairs={{0,16},{16,0},{1,17},{17,1},{2,18},{18,2},{3,19},{19,3},{4,20},{20... | collective-permute-start | bytes 1622024 | tf_op jit(solution)/shard_map/ppermute | solution.py:287
  30.4 1.0 copy-start.1
  31.4 1.0 copy-start.2
  32.4 1.0 copy-start.3
  33.3 1.0 copy-start.4
  62.2 50.0 %all-to-all-start.1 = ((bf16[16,2,64,128]{3,2,1,0:T(8,128)(2,1)}), bf16[16,2,64,128]{3,2,1,0:T(8,128)(2,1)S(1)}, u32[]{:S(2)}, u32[]{:S(2)}) async-start(bf16[16,2,64,128]{3,2,1,0:T(8,128)(2,1)} %get-tuple-element.42), calls=%async_computation.1 | async-start | bytes 1048576 | tf_op jit(solution)/shard_map/all_to_all | solution.py:318
  68.8 4.5 %collective-permute-start.4 = (bf16[2,512,256]{2,1,0:T(8,128)(2,1)S(1)}, bf16[2,512,256]{2,1,0:T(8,128)(2,1)S(1)}, u32[]{:S(2)}, u32[]{:S(2)}) collective-permute-start(bf16[2,512,256]{2,1,0:T(8,128)(2,1)S(1)} %get-tuple-element.33), channel_id=1, source_target_pairs={{0,16},{16,0},{1,17},{17,1},{2,18},{18,2},{3,19},{19,3},{4,20},{20... | collective-permute-start | bytes 1572872 | tf_op jit(solution)/shard_map/ppermute | solution.py:287
  73.5 10.5 %collective-permute-start.5 = (bf16[16,32,256]{2,1,0:T(8,128)(2,1)S(1)}, bf16[16,32,256]{2,1,0:T(8,128)(2,1)S(1)}, u32[]{:S(2)}, u32[]{:S(2)}) collective-permute-start(bf16[16,32,256]{2,1,0:T(8,128)(2,1)S(1)} %get-tuple-element.35), channel_id=1, source_target_pairs={{0,1},{1,0},{2,3},{3,2},{4,5},{5,4},{6,7},{7,6},{8,9},{9,8},{10,11... | collective-permute-start | bytes 786440 | tf_op jit(solution)/shard_map/ppermute | solution.py:143
  84.0 8.4 %collective-permute-start.6 = (bf16[8,32,256]{2,1,0:T(8,128)(2,1)S(1)}, bf16[8,32,256]{2,1,0:T(8,128)(2,1)S(1)}, u32[]{:S(2)}, u32[]{:S(2)}) collective-permute-start(bf16[8,32,256]{2,1,0:T(8,128)(2,1)S(1)} %get-tuple-element.37), channel_id=1, source_target_pairs={{0,2},{1,3},{2,0},{3,1},{4,6},{5,7},{6,4},{7,5},{8,10},{9,11},{10,... | collective-permute-start | bytes 393224 | tf_op jit(solution)/shard_map/ppermute | solution.py:143
  92.4 6.2 %collective-permute-start.7 = (bf16[4,32,256]{2,1,0:T(8,128)(2,1)S(1)}, bf16[4,32,256]{2,1,0:T(8,128)(2,1)S(1)}, u32[]{:S(2)}, u32[]{:S(2)}) collective-permute-start(bf16[4,32,256]{2,1,0:T(8,128)(2,1)S(1)} %get-tuple-element.39), channel_id=1, source_target_pairs={{0,4},{4,0},{8,12},{12,8},{1,5},{5,1},{9,13},{13,9},{2,6},{6,2},{1... | collective-permute-start | bytes 196616 | tf_op jit(solution)/shard_map/ppermute | solution.py:143
  98.5 7.3 %collective-permute-start.8 = (bf16[2,32,256]{2,1,0:T(8,128)(2,1)S(1)}, bf16[2,32,256]{2,1,0:T(8,128)(2,1)S(1)}, u32[]{:S(2)}, u32[]{:S(2)}) collective-permute-start(bf16[2,32,256]{2,1,0:T(8,128)(2,1)S(1)} %get-tuple-element.41), channel_id=1, source_target_pairs={{0,8},{4,12},{8,0},{12,4},{1,9},{5,13},{9,1},{13,5},{2,10},{6,14},... | collective-permute-start | bytes 98312 | tf_op jit(solution)/shard_map/ppermute | solution.py:143
  105.9 5.6 %collective-permute-start.9 = (bf16[32,256]{1,0:T(8,128)(2,1)S(1)}, bf16[32,256]{1,0:T(8,128)(2,1)S(1)}, u32[]{:S(2)}, u32[]{:S(2)}) collective-permute-start(bf16[32,256]{1,0:T(8,128)(2,1)S(1)} %fusion.2), channel_id=1, source_target_pairs={{0,32},{32,0},{64,96},{96,64},{128,160},{160,128},{192,224},{224,1... | collective-permute-start | bytes 49160 | tf_op jit(solution)/shard_map/ppermute | solution.py:291
